TPU v7x, 32 devices: a whole 2x2x4 slice. The times are simulated.
32 devices in a mesh: req: 8 (over z, y), tp: 4 (over x, core).
Axes of the slice: x: 2, y: 2, z: 4, core: 2. Of those that a mesh axis runs over, the one named last changes fastest.
Arguments:
- tokens: bfloat16 [4096, 1536], P(('req', 'tp')), may hold values from -8 to 8
- attention_norm_gain: bfloat16 [1536], replicated, may hold values from 0.5 to 1.5
- expert_norm_gain: bfloat16 [1536], replicated, may hold values from 0.5 to 1.5
- query_projection: bfloat16 [1536, 1536], P(None, 'tp'), may hold values from -1 to 1
- key_projection: bfloat16 [1536, 512], P(None, 'tp'), may hold values from -1 to 1
- value_projection: bfloat16 [1536, 512], P(None, 'tp'), may hold values from -0.15625 to 0.15625
- attention_output_weight: bfloat16 [1536, 1536], P('tp'), may hold values from -0.15625 to 0.15625
- cached_keys: bfloat16 [32768, 512], P('req', 'tp'), may hold values from -6 to 6
- cached_values: bfloat16 [32768, 512], P('req', 'tp'), may hold values from -6 to 6
- token_request: int32 [8, 512], P('req'), may hold values from 0 to 3, never falling along the last dimension, each value on 1 to 256 neighbouring positions
- cached_request: int32 [8, 4096], P('req'), may hold values from 0 to 3, never falling along the last dimension, each value on 1 to 2048 neighbouring positions
- adapter_of_request: int32 [8, 4], P('req'), may hold values from 0 to 63
- adapter_table_row: int32 [64], replicated, may hold values from 0 to 63, each once
- adapter_down_maps: bfloat16 [64, 16, 1536], P('req'), may hold values from -0.15625 to 0.15625
- adapter_query_up: bfloat16 [64, 16, 1536], P('req', None, 'tp'), may hold values from -1.5 to 1.5
- adapter_value_up: bfloat16 [64, 16, 512], P('req', None, 'tp'), may hold values from -1.5 to 1.5
- routes: int32 [4096, 8], P('req'), may hold values from 0 to 31, all different within a row; in each aligned block of 128 rows (0 to 127, 128 to 255, ...) at most 34 rows name the same one
- routed_weight: float32 [4096, 8], P('req'), may hold values from 0.03 to 0.3
- expert_gate_weight: bfloat16 [32, 1536, 512], P('req', None, 'tp'), may hold values from -0.15625 to 0.15625
- expert_up_weight: bfloat16 [32, 1536, 512], P('req', None, 'tp'), may hold values from -0.15625 to 0.15625
- expert_down_weight: bfloat16 [32, 512, 1536], P('req', 'tp'), may hold values from -0.25 to 0.25
Outputs:
- mixed: bfloat16 [4096, 1536], P(('req', 'tp'))
Inputs may be any that keep to these rules, and one draw needn't show every extreme that they name: `routes`: each row names 8 different experts; within each aligned block of 128 rows (the rows of one device) no expert is named by more than 34 rows, a bound that some block reaches. `token_request`: along each row the request numbers never fall; every request has 1 to 256 new tokens and one has exactly that many. `cached_request`: along each row the request numbers never fall; every request has 1 to 2048 cached tokens and one has exactly that many. `adapter_table_row`: each row number of the adapter tables appears once.
All inputs are finite; a program needn't handle non-finite values.
Results may differ from a plain program's by a relative error of at most 0.01.
Values may be sent and summed in bfloat16 or wider, within the bound.
A program may use at most 128 MiB of HBM per device.

v0:
```python
import functools

import jax
import jax.numpy as jnp
from jax import lax
from jax.experimental import pallas as pl
from jax.experimental.pallas import tpu as pltpu
from jax.sharding import PartitionSpec as P

HEAD_SIZE = 64
EXPERTS = 32
TOP = 8
ADAPTER_RANK = 16
GROUP_REQUESTS = 4
LANES = 128
KEY_BLOCK = 512
QUERY_BLOCK = 128
HIDDEN_SCORE = -1e30

norm_eps = 1e-05
rope_theta = 10000.0


def rms_norm(row_block, gain_row):
    values = row_block.astype(jnp.float32)
    inv_rms = lax.rsqrt(jnp.mean(values * values, axis=-1, keepdims=True) + norm_eps)
    return (values * inv_rms * gain_row.astype(jnp.float32)).astype(jnp.bfloat16)


def dot_f32(left, right):
    return jnp.dot(left, right, preferred_element_type=jnp.float32)


def projection_kernel(
    heads, kv_heads, x_ref, gain_ref, wq_ref, wk_ref, wv_ref, down_ref, qup_ref, vup_ref,
    spread_ref, cos_ref, sin_ref, q_ref, k_ref, v_ref
):
    normed = rms_norm(x_ref[...], gain_ref[...])
    low = lax.dot_general(
        normed, down_ref[...], (((1,), (1,)), ((), ())), preferred_element_type=jnp.float32
    )
    low = (low * spread_ref[...]).astype(jnp.bfloat16)
    q = dot_f32(normed, wq_ref[...]) + dot_f32(low, qup_ref[...])
    k = dot_f32(normed, wk_ref[...])
    v_ref[...] = (dot_f32(normed, wv_ref[...]) + dot_f32(low, vup_ref[...])).astype(jnp.bfloat16)
    cosine, sine = cos_ref[...], sin_ref[...]
    lane = lax.broadcasted_iota(jnp.int32, cosine.shape, 1)
    front = lane % HEAD_SIZE < HEAD_SIZE // 2
    upper = lane >= HEAD_SIZE

    def turn(piece):
        partner = jnp.where(
            front,
            pltpu.roll(piece, LANES - HEAD_SIZE // 2, 1),
            pltpu.roll(piece, HEAD_SIZE // 2, 1),
        )
        return piece * cosine + partner * sine

    k_ref[...] = turn(k).astype(jnp.bfloat16)
    per_kv = heads // kv_heads
    for piece_id in range(heads // 2):
        turned = turn(q[:, piece_id * LANES : (piece_id + 1) * LANES]) * HEAD_SIZE ** (-0.5)
        swapped = pltpu.roll(turned, HEAD_SIZE, 1)
        for side in range(2):
            head = 2 * piece_id + side
            kv = head // per_kv
            source = turned if kv == side else swapped
            keep = upper if kv == 1 else jnp.logical_not(upper)
            q_ref[head] = jnp.where(keep, source, 0.0).astype(jnp.bfloat16)


def attention_kernel(
    heads, kv_heads, range_ref, q_ref, ck_ref, cv_ref, nk_ref, nv_ref, bound_ref, wo_ref, out_ref
):
    block = pl.program_id(0)
    rows = q_ref.shape[1]
    queries = q_ref[...].reshape(heads * rows, LANES)
    bounds = jnp.concatenate([bound_ref[...]] * heads, axis=1)
    old_start, old_end, new_start, new_end = (bounds[i : i + 1] for i in range(4))

    def score(keys, first, start, end):
        values = lax.dot_general(
            keys, queries, (((1,), (1,)), ((), ())), preferred_element_type=jnp.float32
        )
        place = lax.broadcasted_iota(jnp.int32, values.shape, 0) + first
        return jnp.where((place >= start) & (place < end), values, HIDDEN_SCORE)

    def gather(weights, values):
        return lax.dot_general(
            values, weights.astype(jnp.bfloat16), (((0,), (0,)), ((), ())),
            preferred_element_type=jnp.float32,
        )

    scores = score(nk_ref[...], 0, new_start, new_end)
    top = jnp.max(scores, axis=0, keepdims=True)
    weights = jnp.exp(scores - top)
    total = jnp.sum(weights, axis=0, keepdims=True)
    mixed = gather(weights, nv_ref[...])

    def step(index, carry):
        top, total, mixed = carry
        first = pl.multiple_of(index * KEY_BLOCK, KEY_BLOCK)
        scores = score(ck_ref[pl.ds(first, KEY_BLOCK), :], first, old_start, old_end)
        new_top = jnp.maximum(top, jnp.max(scores, axis=0, keepdims=True))
        shrink = jnp.exp(top - new_top)
        weights = jnp.exp(scores - new_top)
        total = total * shrink + jnp.sum(weights, axis=0, keepdims=True)
        mixed = mixed * shrink + gather(weights, cv_ref[pl.ds(first, KEY_BLOCK), :])
        return new_top, total, mixed

    top, total, mixed = lax.fori_loop(
        range_ref[0, block], range_ref[1, block], step, (top, total, mixed)
    )
    mixed = mixed / total
    per_kv = heads // kv_heads
    pieces = []
    for piece_id in range(heads // 2):
        halves = []
        for head in (2 * piece_id, 2 * piece_id + 1):
            kv = head // per_kv
            halves.append(
                mixed[kv * HEAD_SIZE : (kv + 1) * HEAD_SIZE, head * rows : (head + 1) * rows]
            )
        pieces.append(jnp.transpose(jnp.concatenate(halves, axis=0)).astype(jnp.bfloat16))
    out_ref[...] = dot_f32(jnp.concatenate(pieces, axis=1), wo_ref[...]).astype(jnp.bfloat16)


def expert_kernel(slots, x_ref, slot_ref, weight_ref, *refs):
    gates, ups, downs = refs[0:4], refs[4:8], refs[8:12]
    out_ref, total_ref = refs[12:]
    expert = pl.program_id(1)
    rows = x_ref.shape[0]
    chosen = lax.broadcasted_iota(jnp.int32, (slots, rows), 0) == slot_ref[0]
    row_weight = jnp.sum(jnp.where(chosen, weight_ref[0], 0.0), axis=1, keepdims=True)
    pick = jnp.where(chosen, 1.0, 0.0).astype(jnp.bfloat16)
    picked = dot_f32(pick, x_ref[...]).astype(jnp.bfloat16)
    gate = dot_f32(picked, jnp.concatenate([ref[0] for ref in gates], axis=1))
    up = dot_f32(picked, jnp.concatenate([ref[0] for ref in ups], axis=1))
    hidden = (jax.nn.silu(gate) * up).astype(jnp.bfloat16)
    result = dot_f32(hidden, jnp.concatenate([ref[0] for ref in downs], axis=0))
    result = (result * row_weight).astype(jnp.bfloat16)
    spread = lax.dot_general(
        pick, result, (((0,), (0,)), ((), ())), preferred_element_type=jnp.float32
    )

    @pl.when(expert == 0)
    def _():
        total_ref[...] = spread

    @pl.when(expert > 0)
    def _():
        total_ref[...] += spread

    @pl.when(expert == pl.num_programs(1) - 1)
    def _():
        out_ref[...] = total_ref[...].astype(jnp.bfloat16)


def on_device(
    tokens,
    attention_norm_gain,
    expert_norm_gain,
    query_projection,
    key_projection,
    value_projection,
    attention_output_weight,
    cached_keys,
    cached_values,
    token_request,
    cached_request,
    adapter_of_request,
    adapter_table_row,
    adapter_down_maps,
    adapter_query_up,
    adapter_value_up,
    routes,
    routed_weight,
    expert_gate_weight,
    expert_up_weight,
    expert_down_weight,
):
    tp_count = lax.axis_size("tp")
    tp_place = lax.axis_index("tp")
    req_count = lax.axis_size("req")
    req_place = lax.axis_index("req")
    own_rows, width = tokens.shape
    group_size = own_rows * tp_count
    query_width = query_projection.shape[1]
    kv_width = key_projection.shape[1]
    heads = query_width // HEAD_SIZE
    kv_heads = kv_width // HEAD_SIZE
    low_rows = GROUP_REQUESTS * ADAPTER_RANK
    assert tp_count == 4 and kv_heads == 2 and own_rows == QUERY_BLOCK
    capacity = own_rows * TOP // EXPERTS + 2

    own_routes = lax.dynamic_slice_in_dim(routes, tp_place * own_rows, own_rows, 0)
    own_gates = lax.dynamic_slice_in_dim(routed_weight, tp_place * own_rows, own_rows, 0)
    wanted_row = jnp.pad(
        adapter_of_request.astype(jnp.float32),
        ((0, 7), (0, own_rows - adapter_of_request.shape[1])),
    )
    notes = jnp.concatenate([own_routes.T.astype(jnp.float32), own_gates.T, wanted_row], axis=0)
    notes = lax.all_gather(notes, "req", axis=0, tiled=False)
    all_routes = notes[:, :TOP].astype(jnp.int32)
    all_gates = notes[:, TOP : 2 * TOP]
    wanted = notes[:, 2 * TOP, :GROUP_REQUESTS].astype(jnp.int32).reshape(-1)

    group_x = lax.all_gather(tokens, "tp", axis=0, tiled=True)

    across = [(i, i ^ 2) for i in range(tp_count)]
    beside = [(i, i ^ 1) for i in range(tp_count)]

    def quarters(piece):
        far = lax.ppermute(piece, "tp", across)
        near = lax.ppermute(piece, "tp", beside)
        far_near = lax.ppermute(far, "tp", beside)
        return [piece, far, near, far_near]

    gates, ups, downs = (
        quarters(expert_gate_weight), quarters(expert_up_weight), quarters(expert_down_weight)
    )

    catalog = jnp.arange(adapter_table_row.shape[0], dtype=jnp.int32)
    table_rows = jnp.sum(
        (wanted[:, None] == catalog[None, :]).astype(jnp.int32) * adapter_table_row[None, :], axis=1
    )
    stored = adapter_down_maps.shape[0]
    local_rows = req_place * stored + jnp.arange(stored, dtype=jnp.int32)
    mine = (table_rows[:, None] == local_rows[None, :])[:, :, None, None]
    down_width = width // tp_count
    down_part = lax.dynamic_slice_in_dim(adapter_down_maps, tp_place * down_width, down_width, 2)

    def select(table):
        return jnp.sum(
            jnp.where(mine, table[None].astype(jnp.float32), 0.0), axis=1
        ).astype(jnp.bfloat16).reshape(-1, table.shape[2])

    adapters = jnp.concatenate(
        [select(down_part), select(adapter_query_up), select(adapter_value_up)], axis=1
    )
    adapters = lax.psum_scatter(adapters, "req", scatter_dimension=0, tiled=True)
    down_selected = lax.all_gather(adapters[:, :down_width], "tp", axis=1, tiled=True)
    query_up_selected = adapters[:, down_width : down_width + query_width]
    value_up_selected = adapters[:, down_width + query_width :]

    new_labels = token_request[0]
    old_labels = cached_request[0]
    labels = jnp.arange(GROUP_REQUESTS, dtype=jnp.int32)
    member = new_labels[:, None] == labels[None, :]
    old_below = jnp.sum((old_labels[:, None] < labels[None, :]).astype(jnp.int32), axis=0)
    old_upto = jnp.sum((old_labels[:, None] <= labels[None, :]).astype(jnp.int32), axis=0)
    new_below = jnp.sum((new_labels[:, None] < labels[None, :]).astype(jnp.int32), axis=0)

    def by_token(table):
        return jnp.sum(jnp.where(member, table[None, :], 0), axis=1)

    place = jnp.arange(group_size, dtype=jnp.int32)
    old_start, old_end, new_start = by_token(old_below), by_token(old_upto), by_token(new_below)
    positions = place - new_start + old_end - old_start
    bounds = jnp.stack([old_start, old_end, new_start, place + 1] * 2, axis=0)
    block_start = jnp.min(old_start.reshape(-1, QUERY_BLOCK), axis=1)
    block_end = jnp.max(old_end.reshape(-1, QUERY_BLOCK), axis=1)
    block_range = jnp.stack(
        [block_start // KEY_BLOCK, (block_end + KEY_BLOCK - 1) // KEY_BLOCK], axis=0
    )
    spread = jnp.repeat(member.astype(jnp.float32), ADAPTER_RANK, axis=1)
    half = HEAD_SIZE // 2
    lane = jnp.arange(LANES, dtype=jnp.int32)
    inverse_freq = rope_theta ** (-((lane % half).astype(jnp.float32) / half))
    angles = positions.astype(jnp.float32)[:, None] * inverse_freq[None, :]
    cosine = jnp.cos(angles)
    sine = jnp.sin(angles) * jnp.where(lane % HEAD_SIZE < half, -1.0, 1.0)[None, :]

    whole = lambda shape: pl.BlockSpec(shape, lambda i, *_: (0,) * len(shape))
    by_row = lambda rows, columns: pl.BlockSpec((rows, columns), lambda i, *_: (i, 0))
    rows = 2 * QUERY_BLOCK
    queries, fresh_keys, fresh_values = pl.pallas_call(
        functools.partial(projection_kernel, heads, kv_heads),
        grid=(group_size // rows,),
        in_specs=[
            by_row(rows, width), whole((1, width)), whole((width, query_width)),
            whole((width, kv_width)), whole((width, kv_width)), whole((low_rows, width)),
            whole((low_rows, query_width)), whole((low_rows, kv_width)), by_row(rows, low_rows),
            by_row(rows, LANES), by_row(rows, LANES),
        ],
        out_specs=[
            pl.BlockSpec((heads, rows, LANES), lambda i: (0, i, 0)),
            by_row(rows, kv_width), by_row(rows, kv_width),
        ],
        out_shape=[
            jax.ShapeDtypeStruct((heads, group_size, LANES), jnp.bfloat16),
            jax.ShapeDtypeStruct((group_size, kv_width), jnp.bfloat16),
            jax.ShapeDtypeStruct((group_size, kv_width), jnp.bfloat16),
        ],
        cost_estimate=pl.CostEstimate(
            flops=2 * group_size * width * (query_width + 2 * kv_width + low_rows),
            bytes_accessed=6_000_000, transcendentals=0,
        ),
        name="projections",
    )(
        group_x, attention_norm_gain[None, :], query_projection, key_projection, value_projection,
        down_selected, query_up_selected, value_up_selected, spread, cosine, sine,
    )

    context = cached_keys.shape[0]
    partial_rows = pl.pallas_call(
        functools.partial(attention_kernel, heads, kv_heads),
        grid_spec=pltpu.PrefetchScalarGridSpec(
            num_scalar_prefetch=1,
            grid=(group_size // QUERY_BLOCK,),
            in_specs=[
                pl.BlockSpec((heads, QUERY_BLOCK, LANES), lambda i, *_: (0, i, 0)),
                whole((context, kv_width)), whole((context, kv_width)),
                whole((group_size, kv_width)), whole((group_size, kv_width)),
                pl.BlockSpec((8, QUERY_BLOCK), lambda i, *_: (0, i)),
                whole((query_width, width)),
            ],
            out_specs=by_row(QUERY_BLOCK, width),
        ),
        out_shape=jax.ShapeDtypeStruct((group_size, width), jnp.bfloat16),
        compiler_params=pltpu.CompilerParams(vmem_limit_bytes=40 << 20),
        cost_estimate=pl.CostEstimate(
            flops=10_000_000_000, bytes_accessed=6_000_000, transcendentals=14_000_000
        ),
        name="attention",
    )(
        block_range, queries, cached_keys, cached_values, fresh_keys, fresh_values, bounds,
        attention_output_weight,
    )
    attn_own = lax.psum_scatter(partial_rows, "tp", scatter_dimension=0, tiled=True)
    resid_own = (tokens.astype(jnp.float32) + attn_own.astype(jnp.float32)).astype(jnp.bfloat16)
    ffn_own = rms_norm(resid_own, expert_norm_gain)
    arrived = lax.all_gather(ffn_own, "req", axis=0, tiled=True)

    local_experts = expert_gate_weight.shape[0]
    total_rows = req_count * own_rows
    chunk_rows = min(8, req_count) * own_rows
    chunk_blocks = chunk_rows // own_rows
    slots = chunk_blocks * capacity
    expert_ids = req_place * local_experts + jnp.arange(local_experts, dtype=jnp.int32)
    hits = all_routes[None] == expert_ids[:, None, None, None]
    expert_weight = jnp.sum(jnp.where(hits, all_gates[None], 0.0), axis=2)
    named = jnp.any(hits, axis=2)
    earlier = jnp.arange(own_rows)[:, None] < jnp.arange(own_rows)[None, :]
    rank = jnp.einsum(
        "ebt,tu->ebu", named.astype(jnp.bfloat16), earlier.astype(jnp.bfloat16),
        preferred_element_type=jnp.float32,
    ).astype(jnp.int32)
    block_base = (jnp.arange(req_count, dtype=jnp.int32) % chunk_blocks) * capacity
    slot_of = jnp.where(named, rank + block_base[None, :, None], -1)
    slot_of = slot_of.reshape(local_experts, 1, total_rows)
    expert_weight = expert_weight.reshape(local_experts, 1, total_rows)

    quarter = expert_gate_weight.shape[2]
    row_spec = pl.BlockSpec((1, 1, chunk_rows), lambda c, e: (e, 0, c))
    moe = pl.pallas_call(
        functools.partial(expert_kernel, slots),
        grid=(total_rows // chunk_rows, local_experts),
        in_specs=[pl.BlockSpec((chunk_rows, width), lambda c, e: (c, 0)), row_spec, row_spec]
        + [pl.BlockSpec((1, width, quarter), lambda c, e: (e, 0, 0))] * 8
        + [pl.BlockSpec((1, quarter, width), lambda c, e: (e, 0, 0))] * 4,
        out_specs=pl.BlockSpec((chunk_rows, width), lambda c, e: (c, 0)),
        out_shape=jax.ShapeDtypeStruct((total_rows, width), jnp.bfloat16),
        scratch_shapes=[pltpu.VMEM((chunk_rows, width), jnp.float32)],
        compiler_params=pltpu.CompilerParams(vmem_limit_bytes=52 << 20),
        cost_estimate=pl.CostEstimate(
            flops=12_000_000_000, bytes_accessed=26_000_000, transcendentals=600_000
        ),
        name="experts",
    )(arrived, slot_of, expert_weight, *gates, *ups, *downs)
    moe_own = lax.psum_scatter(moe, "req", scatter_dimension=0, tiled=True)
    return (resid_own.astype(jnp.float32) + moe_own.astype(jnp.float32)).astype(jnp.bfloat16)


def solution(mesh):
    return jax.shard_map(
        on_device,
        mesh=mesh,
        in_specs=(
            P(("req", "tp"), None),
            P(),
            P(),
            P(None, "tp"),
            P(None, "tp"),
            P(None, "tp"),
            P("tp", None),
            P("req", "tp"),
            P("req", "tp"),
            P("req", None),
            P("req", None),
            P("req", None),
            P(),
            P("req", None, None),
            P("req", None, "tp"),
            P("req", None, "tp"),
            P("req", None),
            P("req", None),
            P("req", None, "tp"),
            P("req", None, "tp"),
            P("req", "tp", None),
        ),
        out_specs=P(("req", "tp"), None),
        check_vma=False,
    )
```

profile of v0, /device:TPU:0, one launch (start us, length us, event | category | flops | bytes accessed | tf_op | source)
XLA Modules:
  0.0 400.8 jit_solution(4282318620540661490)
XLA Ops:
  9.5 32.3 %all-gather = f32[192,128]{1,0:T(8,128)S(1)} all-gather(f32[24,128]{1,0:T(8,128)S(1)} %select_maximum_fusion), channel_id=2, replica_groups=mesh['req'=8,'tp'=4] {'req'}, dimensions={0}, use_global_device_ids=true | all-gather | bytes 110592 | tf_op jit(solution)/shard_map/all_gather | solution.py:203
  44.1 0.9 dynamic-slice_convert_fusion
  45.1 1.9 select_reduce_fusion.1
  47.0 1.0 pad_maximum_fusion
  50.9 1.8 fusion.6
  52.7 59.3 %reduce-scatter.4.cloned.1.call-done = bf16[64,896]{1,0:T(8,128)(2,1)} async-done(((bf16[512,896]{1,0:T(8,128)(2,1)}), bf16[64,896]{1,0:T(8,128)(2,1)}) %reduce-scatter.4.cloned.1.call-update) | async-done | bytes 114704 | tf_op jit(solution)/shard_map/reduce_scatter | solution.py:241
  112.0 1.3 slice.27.vup_ref
  113.4 1.4 fusion.16
  114.8 6.1 %all_gather.18.down_ref = bf16[64,1536]{1,0:T(8,128)(2,1)} all-gather(bf16[64,384]{1,0:T(8,128)(2,1)S(1)} %get-tuple-element.19), channel_id=1, replica_groups=mesh['req'=8,'tp'=4] {'tp'}, dimensions={1}, use_global_device_ids=true | all-gather | bytes 245760 | tf_op jit(solution)/shard_map/all_gather | solution.py:242
  120.9 6.7 %projections.1 = (bf16[6,512,128]{2,1,0:T(8,128)(2,1)}, bf16[512,128]{1,0:T(8,128)(2,1)}, bf16[512,128]{1,0:T(8,128)(2,1)}) custom-call(bf16[512,1536]{1,0:T(8,128)(2,1)} %all-gather.4.cloned.1.call-done.x_ref, bf16[1,1536]{1,0:T(2,128)(2,1)} %broadcast_in_dim.132.gain_ref, bf16[1536,384]{1,0:T(8,128)(2,1)} %wq_ref.1, bf16[1536,128]{1,0:T(8,128)(2,1)} %wk_ref.1, ...), custom_call_target="tpu_custom_call" | custom-call | flops 1107296256 | bytes 6000000 | tf_op jit(solution)/shard_map/projections/pallas_call | solution.py:277
  127.6 1.1 copy-done.5
  130.6 17.1 %attention.1 = bf16[512,1536]{1,0:T(8,128)(2,1)} custom-call(s32[2,4]{1,0:T(2,128)S(1)} %pad_add_fusion.range_ref, bf16[6,512,128]{2,1,0:T(8,128)(2,1)S(1)} %copy-done.5, bf16[4096,128]{1,0:T(8,128)(2,1)S(1)} %copy-done.3, bf16[4096,128]{1,0:T(8,128)(2,1)S(1)} %copy-done.4, bf16[512,128]{1,0:T(8,128)(2,1)S(1)} %copy-done.6, bf16[512,128]{1,0:T(8,128)(2,1)S(1)} %copy-done.7, ...), custom_call_target="tpu_custom_call" | custom-call | flops 10000000000 | bytes 6000000 | tf_op jit(solution)/shard_map/attention/pallas_call | solution.py:306
  148.4 33.4 %reduce-scatter.6.cloned.1.call-done = bf16[128,1536]{1,0:T(8,128)(2,1)} async-done(((bf16[512,1536]{1,0:T(8,128)(2,1)}), bf16[128,1536]{1,0:T(8,128)(2,1)}) %reduce-scatter.6.cloned.1.call-update) | async-done | bytes 393232 | tf_op jit(solution)/shard_map/reduce_scatter | solution.py:330
  181.8 1.2 fusion.2
  183.0 1.9 fusion.4
  185.6 1.7 collective-permute-start.3
  187.7 35.0 %collective-permute-done.refs_1_ = bf16[4,1536,128]{2,1,0:T(8,128)(2,1)} collective-permute-done((bf16[4,1536,128]{2,1,0:T(8,128)(2,1)S(1)}, bf16[4,1536,128]{2,1,0:T(8,128)(2,1)}, u32[]{:S(2)}, u32[]{:S(2)}) %collective-permute-start) | collective-permute-done | bytes 1572896 | tf_op jit(solution)/shard_map/ppermute | solution.py:214
  222.7 1.2 copy-done.14
  224.4 32.0 %collective-permute-done.3.refs_5_ = bf16[4,1536,128]{2,1,0:T(8,128)(2,1)} collective-permute-done((bf16[4,1536,128]{2,1,0:T(8,128)(2,1)}, bf16[4,1536,128]{2,1,0:T(8,128)(2,1)}, u32[]{:S(2)}, u32[]{:S(2)}) %collective-permute-start.3) | collective-permute-done | bytes 1572896 | tf_op jit(solution)/shard_map/ppermute | solution.py:214
  256.4 32.5 %collective-permute-done.6.refs_9_ = bf16[4,128,1536]{2,1,0:T(8,128)(2,1)} collective-permute-done((bf16[4,128,1536]{2,1,0:T(8,128)(2,1)}, bf16[4,128,1536]{2,1,0:T(8,128)(2,1)}, u32[]{:S(2)}, u32[]{:S(2)}) %collective-permute-start.6) | collective-permute-done | bytes 1572896 | tf_op jit(solution)/shard_map/ppermute | solution.py:214
  289.3 3.3 collective-permute-done.8.refs_11_
  292.6 24.6 %experts.1 = bf16[1024,1536]{1,0:T(8,128)(2,1)} custom-call(bf16[1024,1536]{1,0:T(8,128)(2,1)} %all-gather.6.cloned.1.call-done.x_ref, s32[4,1,1024]{2,1,0:T(1,128)S(1)} %bitcast.44, f32[4,1,1024]{2,1,0:T(1,128)S(1)} %bitcast.43, bf16[4,1536,128]{2,1,0:T(8,128)(2,1)S(1)} %copy-done.1, bf16[4,1536,128]{2,1,0:T(8,128)(2,1)} %collective-permute-done.refs_1_, ...), custom_call_target="tpu_custom_call" | custom-call | flops 12000000000 | bytes 26000000 | tf_op jit(solution)/shard_map/experts/pallas_call | solution.py:356
  317.2 74.6 %reduce-scatter.8.cloned.1.call-done = bf16[128,1536]{1,0:T(8,128)(2,1)} async-done(((bf16[1024,1536]{1,0:T(8,128)(2,1)}), bf16[128,1536]{1,0:T(8,128)(2,1)}) %reduce-scatter.8.cloned.1.call-update) | async-done | bytes 393232 | tf_op jit(solution)/shard_map/reduce_scatter | solution.py:371
  391.8 1.9 fusion.5
  (89 shorter events, 11.7 us)
Async XLA Ops:
  7.4 1.4 copy-start
  7.4 104.7 %reduce-scatter.4.cloned.1.call-start = ((), (), s32[]{:S(2)}) async-start(), calls=%async_computation.4 | async-start | bytes 1032192 | tf_op jit(solution)/shard_map/reduce_scatter | solution.py:241
  47.0 1.7 copy-start.13
  47.0 2.3 copy-start.10
  47.0 3.3 copy-start.11
  48.0 72.8 %all-gather.4.cloned.1.call-start = ((), (), s32[]{:S(2)}) async-start(), calls=%async_computation.3 | async-start | bytes 1966080 | tf_op jit(solution)/shard_map/all_gather | solution.py:208
  48.6 133.2 %reduce-scatter.6.cloned.1.call-start = ((), (), s32[]{:S(2)}) async-start(), calls=%async_computation.5 | async-start | bytes 1966080 | tf_op jit(solution)/shard_map/reduce_scatter | solution.py:330
  120.9 6.7 %copy-start.2 = (bf16[384,1536]{1,0:T(8,128)(2,1)S(1)}, bf16[384,1536]{1,0:T(8,128)(2,1)}, u32[]{:S(2)}) copy-start(bf16[384,1536]{1,0:T(8,128)(2,1)} %wo_ref.1) | copy-start | bytes 3538948
  120.9 6.7 %copy-start.3 = (bf16[4096,128]{1,0:T(8,128)(2,1)S(1)}, bf16[4096,128]{1,0:T(8,128)(2,1)}, u32[]{:S(2)}) copy-start(bf16[4096,128]{1,0:T(8,128)(2,1)} %ck_ref.1) | copy-start | bytes 3145732
  120.9 6.7 %copy-start.4 = (bf16[4096,128]{1,0:T(8,128)(2,1)S(1)}, bf16[4096,128]{1,0:T(8,128)(2,1)}, u32[]{:S(2)}) copy-start(bf16[4096,128]{1,0:T(8,128)(2,1)} %cv_ref.1) | copy-start | bytes 3145732
  147.7 34.1 %copy-start.8 = (bf16[128,1536]{1,0:T(8,128)(2,1)S(1)}, bf16[128,1536]{1,0:T(8,128)(2,1)}, u32[]{:S(2)}) copy-start(bf16[128,1536]{1,0:T(8,128)(2,1)} %param.21) | copy-start | bytes 1179652
  147.7 37.5 %copy-start.1 = (bf16[4,1536,128]{2,1,0:T(8,128)(2,1)S(1)}, bf16[4,1536,128]{2,1,0:T(8,128)(2,1)}, u32[]{:S(2)}) copy-start(bf16[4,1536,128]{2,1,0:T(8,128)(2,1)} %refs_0_.1) | copy-start | bytes 4718596
  147.7 144.9 %all-gather.6.cloned.1.call-start = ((), (), s32[]{:S(2)}) async-start(), calls=%async_computation.6 | async-start | bytes 3538944 | tf_op jit(solution)/shard_map/all_gather | solution.py:333
  185.0 206.9 %reduce-scatter.8.cloned.1.call-start = ((), (), s32[]{:S(2)}) async-start(), calls=%async_computation.7 | async-start | bytes 3538944 | tf_op jit(solution)/shard_map/reduce_scatter | solution.py:371
  185.2 37.5 %collective-permute-start = (bf16[4,1536,128]{2,1,0:T(8,128)(2,1)S(1)}, bf16[4,1536,128]{2,1,0:T(8,128)(2,1)}, u32[]{:S(2)}, u32[]{:S(2)}) collective-permute-start(bf16[4,1536,128]{2,1,0:T(8,128)(2,1)S(1)} %copy-done.1), channel_id=1, source_target_pairs={{0,2},{1,3},{2,0},{3,1},{4,6},{5,7},{6,4},{7,5},{8,10},{9,11},{10,... | collective-permute-start | bytes 4718600 | tf_op jit(solution)/shard_map/ppermute | solution.py:214
  185.6 37.1 %collective-permute-start.1 = (bf16[4,1536,128]{2,1,0:T(8,128)(2,1)S(1)}, bf16[4,1536,128]{2,1,0:T(8,128)(2,1)S(1)}, u32[]{:S(2)}, u32[]{:S(2)}) collective-permute-start(bf16[4,1536,128]{2,1,0:T(8,128)(2,1)S(1)} %copy-done.1), channel_id=1, source_target_pairs={{0,1},{1,0},{2,3},{3,2},{4,5},{5,4},{6,7},{7,6},{8,9},{9,8},{10,11... | collective-permute-start | bytes 4718600 | tf_op jit(solution)/shard_map/ppermute | solution.py:215
  185.6 70.8 %collective-permute-start.3 = (bf16[4,1536,128]{2,1,0:T(8,128)(2,1)}, bf16[4,1536,128]{2,1,0:T(8,128)(2,1)}, u32[]{:S(2)}, u32[]{:S(2)}) collective-permute-start(bf16[4,1536,128]{2,1,0:T(8,128)(2,1)} %refs_4_.1), channel_id=1, source_target_pairs={{0,2},{1,3},{2,0},{3,1},{4,6},{5,7},{6,4},{7,5},{8,10},{9,11},{10,... | collective-permute-start | bytes 4718600 | tf_op jit(solution)/shard_map/ppermute | solution.py:214
  187.3 101.5 %collective-permute-start.6 = (bf16[4,128,1536]{2,1,0:T(8,128)(2,1)}, bf16[4,128,1536]{2,1,0:T(8,128)(2,1)}, u32[]{:S(2)}, u32[]{:S(2)}) collective-permute-start(bf16[4,128,1536]{2,1,0:T(8,128)(2,1)} %refs_8_.1), channel_id=1, source_target_pairs={{0,2},{1,3},{2,0},{3,1},{4,6},{5,7},{6,4},{7,5},{8,10},{9,11},{10,... | collective-permute-start | bytes 4718600 | tf_op jit(solution)/shard_map/ppermute | solution.py:214
  187.6 101.6 %collective-permute-start.4 = (bf16[4,1536,128]{2,1,0:T(8,128)(2,1)}, bf16[4,1536,128]{2,1,0:T(8,128)(2,1)}, u32[]{:S(2)}, u32[]{:S(2)}) collective-permute-start(bf16[4,1536,128]{2,1,0:T(8,128)(2,1)} %refs_4_.1), channel_id=1, source_target_pairs={{0,1},{1,0},{2,3},{3,2},{4,5},{5,4},{6,7},{7,6},{8,9},{9,8},{10,11... | collective-permute-start | bytes 4718600 | tf_op jit(solution)/shard_map/ppermute | solution.py:215
  222.7 66.6 %collective-permute-start.7 = (bf16[4,128,1536]{2,1,0:T(8,128)(2,1)}, bf16[4,128,1536]{2,1,0:T(8,128)(2,1)}, u32[]{:S(2)}, u32[]{:S(2)}) collective-permute-start(bf16[4,128,1536]{2,1,0:T(8,128)(2,1)} %refs_8_.1), channel_id=1, source_target_pairs={{0,1},{1,0},{2,3},{3,2},{4,5},{5,4},{6,7},{7,6},{8,9},{9,8},{10,11... | collective-permute-start | bytes 4718600 | tf_op jit(solution)/shard_map/ppermute | solution.py:215
  223.9 65.4 %collective-permute-start.2 = (bf16[4,1536,128]{2,1,0:T(8,128)(2,1)}, bf16[4,1536,128]{2,1,0:T(8,128)(2,1)}, u32[]{:S(2)}, u32[]{:S(2)}) collective-permute-start(bf16[4,1536,128]{2,1,0:T(8,128)(2,1)} %collective-permute-done.refs_1_), channel_id=1, source_target_pairs={{0,1},{1,0},{2,3},{3,2},{4,5},{5,4},{6,7},{7,6},{8,9},{9,8},{10,11... | collective-permute-start | bytes 4718600 | tf_op jit(solution)/shard_map/ppermute | solution.py:216
  256.4 32.9 %collective-permute-start.5 = (bf16[4,1536,128]{2,1,0:T(8,128)(2,1)}, bf16[4,1536,128]{2,1,0:T(8,128)(2,1)}, u32[]{:S(2)}, u32[]{:S(2)}) collective-permute-start(bf16[4,1536,128]{2,1,0:T(8,128)(2,1)} %collective-permute-done.3.refs_5_), channel_id=1, source_target_pairs={{0,1},{1,0},{2,3},{3,2},{4,5},{5,4},{6,7},{7,6},{8,9},{9,8},{10,11... | collective-permute-start | bytes 4718600 | tf_op jit(solution)/shard_map/ppermute | solution.py:216
  288.8 3.8 collective-permute-start.8
  317.2 74.6 %copy-start.9 = (bf16[128,1536]{1,0:T(8,128)(2,1)S(1)}, bf16[128,1536]{1,0:T(8,128)(2,1)}, u32[]{:S(2)}) copy-start(bf16[128,1536]{1,0:T(8,128)(2,1)} %reduce-scatter.6.cloned.1.call-done) | copy-start | bytes 1179652
  (5 other events, 4.9 us)
Sparse Core Ops, SparseCore 0:
  48.2 63.8 reduce-scatter.3
  185.1 60.4 all-gather.5
  317.4 74.4 reduce-scatter.7
Sparse Core Ops, SparseCore 1:
  50.1 20.4 all-gather.3
  147.8 34.0 reduce-scatter.5
where the time goes:
time: 402 us; the launch traced here: 401 us
  waiting for transfers between devices  271 us (67%)
  Pallas kernels  48.5 us (12%)
  blocking collectives  38.4 us (10%)
  other arithmetic  15.9 us (4%)
  between operations  14.8 us (4%)
  local copies, waits for them, and re-layouts  9.15 us (2%)
    ppermute x3, waiting for transfers between devices, quarters(): far = lax.ppermute(piece, 'tp', across)  99.4 us
    reduce_scatter x1, waiting for transfers between devices, on_device(): moe_own = lax.psum_scatter(moe, 'req', scatter_dimension=0, tiled=True)  74.6 us
    reduce_scatter x1, waiting for transfers between devices, on_device(): lax.psum_scatter(adapters, 'req', scatter_dimension=0, tiled=True)  59.3 us
    reduce_scatter x1, waiting for transfers between devices, on_device(): lax.psum_scatter(partial_rows, 'tp', scatter_dimension=0, tiled=True)  33.4 us
    all_gather x1, blocking collectives, on_device(): notes = lax.all_gather(notes, 'req', axis=0, tiled=False)  32.3 us
    pallas_call x1, Pallas kernels, on_device(): pl.pallas_call(functools.partial(expert_kernel, slots), grid=(total_rows...  24.6 us
    pallas_call x1, Pallas kernels, on_device(): pl.pallas_call(functools.partial(attention_kernel, heads, kv_heads), grid...  17.1 us
  transfers between devices with their start and end apart: 14, of which 7 were waited for; matrix products, arithmetic and copies ran while one was open for 2% of the time, Pallas kernels for 0%

commit v1 on v0

--- a/solution.py
+++ b/solution.py
@@ -154,6 +154,195 @@
     @pl.when(expert == pl.num_programs(1) - 1)
     def _():
         out_ref[...] = total_ref[...].astype(jnp.bfloat16)
+
+
+MESH = pl.DeviceIdType.MESH
+
+
+def send_to(source, target, send_sem, recv_sem, axis, device):
+    return pltpu.make_async_remote_copy(
+        src_ref=source, dst_ref=target, send_sem=send_sem, recv_sem=recv_sem,
+        device_id={axis: device}, device_id_type=MESH,
+    )
+
+
+def greet(peers):
+    barrier = pltpu.get_barrier_semaphore()
+    for axis, device in peers:
+        pl.semaphore_signal(barrier, inc=1, device_id={axis: device}, device_id_type=MESH)
+    pl.semaphore_wait(barrier, len(peers))
+
+
+def core_partner(place):
+    return place + 1 - 2 * (place % 2)
+
+
+def opening_kernel(
+    req_count, tp_count, stored, tokens_ref, notes_ref, table_ref,
+    group_ref, all_notes_ref, down_ref, qup_ref, vup_ref,
+    noted, chosen, arrived, own_down, downs,
+    local_sem, x_send, x_recv, n_send, n_recv, a_send, a_recv, d_send, d_recv
+):
+    me, here = lax.axis_index("req"), lax.axis_index("tp")
+    beside, across = core_partner(here), (here + 2) % tp_count
+    greet(
+        [("req", (me + step) % req_count) for step in range(1, req_count)]
+        + [("tp", (here + step) % tp_count) for step in range(1, tp_count)]
+    )
+    note_copies = []
+    for step in range(1, req_count):
+        copy = send_to(notes_ref, noted.at[step], n_send.at[step], n_recv.at[step], "req",
+                       (me + step) % req_count)
+        copy.start()
+        note_copies.append(copy)
+    own_copy = pltpu.make_async_copy(tokens_ref, group_ref.at[here], local_sem)
+    own_copy.start()
+    to_across = send_to(tokens_ref, group_ref.at[here], x_send.at[0], x_recv.at[0], "tp", across)
+    to_across.start()
+    to_beside = send_to(tokens_ref, group_ref.at[here], x_send.at[1], x_recv.at[1], "tp", beside)
+    to_beside.start()
+
+    rows = GROUP_REQUESTS * ADAPTER_RANK
+    depth = stored * ADAPTER_RANK
+    lane = lax.broadcasted_iota(jnp.int32, (rows, depth), 1)
+    row = lax.broadcasted_iota(jnp.int32, (rows, depth), 0)
+    same_rank = lane % ADAPTER_RANK == row % ADAPTER_RANK
+    slot = (me * stored + lane // ADAPTER_RANK).astype(jnp.float32)
+
+    def select(notes):
+        wanted = notes[2 * TOP :, :depth]
+        pick = jnp.where(same_rank & (wanted == slot), 1.0, 0.0).astype(jnp.bfloat16)
+        return dot_f32(pick, table_ref[...])
+
+    total = select(notes_ref[...])
+    all_notes_ref[me] = notes_ref[: 2 * TOP, :]
+    adapter_copies = []
+    for step in range(1, req_count):
+        note_copies[step - 1].wait()
+        notes = noted[step]
+        source = (me + req_count - step) % req_count
+        all_notes_ref[source] = notes[: 2 * TOP, :]
+        chosen[step] = select(notes).astype(jnp.bfloat16)
+        copy = send_to(chosen.at[step], arrived.at[step], a_send.at[step], a_recv.at[step], "req",
+                       source)
+        copy.start()
+        adapter_copies.append(copy)
+    to_across.wait()
+    forward = send_to(group_ref.at[across], group_ref.at[across], x_send.at[2], x_recv.at[2], "tp",
+                      beside)
+    forward.start()
+    for step in range(1, req_count):
+        adapter_copies[step - 1].wait()
+        total = total + arrived[step].astype(jnp.float32)
+    total = total.astype(jnp.bfloat16)
+    down_width = own_down.shape[1]
+    query_width = qup_ref.shape[1]
+    own_down[...] = total[:, :down_width]
+    downs[here] = total[:, :down_width]
+    down_copies = []
+    for step in range(1, tp_count):
+        copy = send_to(own_down, downs.at[here], d_send.at[step], d_recv.at[step], "tp",
+                       (here + step) % tp_count)
+        copy.start()
+        down_copies.append(copy)
+    qup_ref[...] = total[:, down_width : down_width + query_width]
+    vup_ref[...] = total[:, down_width + query_width :]
+    for copy in down_copies:
+        copy.wait()
+    down_ref[...] = jnp.concatenate([downs[i] for i in range(tp_count)], axis=1)
+    own_copy.wait()
+    to_beside.wait()
+    forward.wait()
+
+
+def middle_kernel(
+    req_count, tp_count, partial_ref, tokens_ref, gain_ref, resid_ref, arrived_ref,
+    pair, joined, far, ffn, local_sem, p_send, p_recv, z_send, z_recv, f_send, f_recv
+):
+    me, here = lax.axis_index("req"), lax.axis_index("tp")
+    beside, across = core_partner(here), (here + 2) % tp_count
+    partner = core_partner(me)
+    line = req_count // 2
+    greet(
+        [("tp", beside), ("tp", across), ("req", partner)]
+        + [("req", (me + 2 * step) % req_count) for step in range(1, line)]
+    )
+    f32 = jnp.float32
+    second = send_to(partial_ref.at[(beside + 2) % tp_count], pair.at[1], p_send.at[1],
+                     p_recv.at[1], "tp", beside)
+    second.start()
+    first = send_to(partial_ref.at[beside], pair.at[0], p_send.at[0], p_recv.at[0], "tp", beside)
+    first.start()
+    second.wait()
+    joined[...] = (partial_ref[across].astype(f32) + pair[1].astype(f32)).astype(jnp.bfloat16)
+    last = send_to(joined, far, p_send.at[2], p_recv.at[2], "tp", across)
+    last.start()
+    first.wait()
+    own = partial_ref[here].astype(f32) + pair[0].astype(f32) + tokens_ref[...].astype(f32)
+    last.wait()
+    resid = (own + far[...].astype(f32)).astype(jnp.bfloat16)
+    resid_ref[...] = resid
+    ffn[...] = rms_norm(resid, gain_ref[...])
+    line_copies = []
+    for step in range(1, line):
+        copy = send_to(ffn, arrived_ref.at[me], z_send.at[step], z_recv.at[step], "req",
+                       (me + 2 * step) % req_count)
+        copy.start()
+        line_copies.append(copy)
+    to_partner = send_to(ffn, arrived_ref.at[me], f_send.at[0], f_recv.at[0], "req", partner)
+    to_partner.start()
+    own_copy = pltpu.make_async_copy(ffn, arrived_ref.at[me], local_sem)
+    own_copy.start()
+    forwards = []
+    for step in range(1, line):
+        line_copies[step - 1].wait()
+        source = (me + req_count - 2 * step) % req_count
+        copy = send_to(arrived_ref.at[source], arrived_ref.at[source], f_send.at[step],
+                       f_recv.at[step], "req", partner)
+        copy.start()
+        forwards.append(copy)
+    own_copy.wait()
+    to_partner.wait()
+    for copy in forwards:
+        copy.wait()
+
+
+def closing_kernel(
+    req_count, moe_ref, resid_ref, out_ref, beside_in, line_out, line_in,
+    y_send, y_recv, z_send, z_recv
+):
+    me = lax.axis_index("req")
+    partner = core_partner(me)
+    line = req_count // 2
+    greet(
+        [("req", partner)]
+        + [("req", (me + 2 * step) % req_count) for step in range(1, line)]
+    )
+    f32 = jnp.float32
+    order = list(range(1, line)) + [0]
+    beside_copies = {}
+    for step in order:
+        copy = send_to(moe_ref.at[(partner + 2 * step) % req_count], beside_in.at[step],
+                       y_send.at[step], y_recv.at[step], "req", partner)
+        copy.start()
+        beside_copies[step] = copy
+    line_copies = []
+    for step in range(1, line):
+        target = (me + 2 * step) % req_count
+        beside_copies[step].wait()
+        line_out[step] = (
+            moe_ref[target].astype(f32) + beside_in[step].astype(f32)
+        ).astype(jnp.bfloat16)
+        copy = send_to(line_out.at[step], line_in.at[step], z_send.at[step], z_recv.at[step],
+                       "req", target)
+        copy.start()
+        line_copies.append(copy)
+    beside_copies[0].wait()
+    total = resid_ref[...].astype(f32) + moe_ref[me].astype(f32) + beside_in[0].astype(f32)
+    for step in range(1, line):
+        line_copies[step - 1].wait()
+        total = total + line_in[step].astype(f32)
+    out_ref[...] = total.astype(jnp.bfloat16)
 
 
 def on_device(
@@ -195,53 +384,70 @@
 
     own_routes = lax.dynamic_slice_in_dim(routes, tp_place * own_rows, own_rows, 0)
     own_gates = lax.dynamic_slice_in_dim(routed_weight, tp_place * own_rows, own_rows, 0)
-    wanted_row = jnp.pad(
-        adapter_of_request.astype(jnp.float32),
-        ((0, 7), (0, own_rows - adapter_of_request.shape[1])),
-    )
-    notes = jnp.concatenate([own_routes.T.astype(jnp.float32), own_gates.T, wanted_row], axis=0)
-    notes = lax.all_gather(notes, "req", axis=0, tiled=False)
-    all_routes = notes[:, :TOP].astype(jnp.int32)
-    all_gates = notes[:, TOP : 2 * TOP]
-    wanted = notes[:, 2 * TOP, :GROUP_REQUESTS].astype(jnp.int32).reshape(-1)
-
-    group_x = lax.all_gather(tokens, "tp", axis=0, tiled=True)
+    catalog = jnp.arange(adapter_table_row.shape[0], dtype=jnp.int32)
+    table_rows = jnp.sum(
+        (adapter_of_request[0][:, None] == catalog[None, :]).astype(jnp.int32)
+        * adapter_table_row[None, :],
+        axis=1,
+    )
+    wanted = jnp.broadcast_to(
+        jnp.repeat(table_rows, ADAPTER_RANK).astype(jnp.float32)[:, None], (low_rows, LANES)
+    )
+    notes = jnp.concatenate([own_routes.T.astype(jnp.float32), own_gates.T, wanted], axis=0)
 
     across = [(i, i ^ 2) for i in range(tp_count)]
     beside = [(i, i ^ 1) for i in range(tp_count)]
 
-    def quarters(piece):
-        far = lax.ppermute(piece, "tp", across)
+    gate_far, up_far, down_far = (
+        lax.ppermute(piece, "tp", across)
+        for piece in (expert_gate_weight, expert_up_weight, expert_down_weight)
+    )
+
+    def quarters(piece, far):
         near = lax.ppermute(piece, "tp", beside)
-        far_near = lax.ppermute(far, "tp", beside)
-        return [piece, far, near, far_near]
-
-    gates, ups, downs = (
-        quarters(expert_gate_weight), quarters(expert_up_weight), quarters(expert_down_weight)
-    )
-
-    catalog = jnp.arange(adapter_table_row.shape[0], dtype=jnp.int32)
-    table_rows = jnp.sum(
-        (wanted[:, None] == catalog[None, :]).astype(jnp.int32) * adapter_table_row[None, :], axis=1
-    )
+        return [piece, far, near, lax.ppermute(far, "tp", beside)]
+
     stored = adapter_down_maps.shape[0]
-    local_rows = req_place * stored + jnp.arange(stored, dtype=jnp.int32)
-    mine = (table_rows[:, None] == local_rows[None, :])[:, :, None, None]
     down_width = width // tp_count
     down_part = lax.dynamic_slice_in_dim(adapter_down_maps, tp_place * down_width, down_width, 2)
-
-    def select(table):
-        return jnp.sum(
-            jnp.where(mine, table[None].astype(jnp.float32), 0.0), axis=1
-        ).astype(jnp.bfloat16).reshape(-1, table.shape[2])
-
-    adapters = jnp.concatenate(
-        [select(down_part), select(adapter_query_up), select(adapter_value_up)], axis=1
-    )
-    adapters = lax.psum_scatter(adapters, "req", scatter_dimension=0, tiled=True)
-    down_selected = lax.all_gather(adapters[:, :down_width], "tp", axis=1, tiled=True)
-    query_up_selected = adapters[:, down_width : down_width + query_width]
-    value_up_selected = adapters[:, down_width + query_width :]
+    table = jnp.concatenate([down_part, adapter_query_up, adapter_value_up], axis=2)
+    adapter_width = table.shape[2]
+    table = table.reshape(stored * ADAPTER_RANK, adapter_width)
+    in_vmem = pl.BlockSpec(memory_space=pltpu.VMEM)
+    in_place = pl.BlockSpec(memory_space=pl.ANY)
+    dma = pltpu.SemaphoreType.DMA
+    bf16 = jnp.bfloat16
+    group_x, notes, down_selected, query_up_selected, value_up_selected = pl.pallas_call(
+        functools.partial(opening_kernel, req_count, tp_count, stored),
+        in_specs=[in_vmem] * 3,
+        out_specs=[in_place] + [in_vmem] * 4,
+        out_shape=[
+            jax.ShapeDtypeStruct((tp_count, own_rows, width), bf16),
+            jax.ShapeDtypeStruct((req_count, 2 * TOP, own_rows), jnp.float32),
+            jax.ShapeDtypeStruct((low_rows, width), bf16),
+            jax.ShapeDtypeStruct((low_rows, query_width), bf16),
+            jax.ShapeDtypeStruct((low_rows, kv_width), bf16),
+        ],
+        scratch_shapes=[
+            pltpu.VMEM((req_count,) + notes.shape, jnp.float32),
+            pltpu.VMEM((req_count, low_rows, adapter_width), bf16),
+            pltpu.VMEM((req_count, low_rows, adapter_width), bf16),
+            pltpu.VMEM((low_rows, down_width), bf16),
+            pltpu.VMEM((tp_count, low_rows, down_width), bf16),
+            dma, dma((3,)), dma((3,)), dma((req_count,)), dma((req_count,)),
+            dma((req_count,)), dma((req_count,)), dma((tp_count,)), dma((tp_count,)),
+        ],
+        compiler_params=pltpu.CompilerParams(
+            collective_id=1, has_side_effects=True, vmem_limit_bytes=32 << 20
+        ),
+        cost_estimate=pl.CostEstimate(
+            flops=0, bytes_accessed=90_000_000, transcendentals=0
+        ),
+        name="opening",
+    )(tokens, notes, table)
+    group_x = group_x.reshape(group_size, width)
+    all_routes = notes[:, :TOP].astype(jnp.int32)
+    all_gates = notes[:, TOP:]
 
     new_labels = token_request[0]
     old_labels = cached_request[0]
@@ -327,10 +533,34 @@
         block_range, queries, cached_keys, cached_values, fresh_keys, fresh_values, bounds,
         attention_output_weight,
     )
-    attn_own = lax.psum_scatter(partial_rows, "tp", scatter_dimension=0, tiled=True)
-    resid_own = (tokens.astype(jnp.float32) + attn_own.astype(jnp.float32)).astype(jnp.bfloat16)
-    ffn_own = rms_norm(resid_own, expert_norm_gain)
-    arrived = lax.all_gather(ffn_own, "req", axis=0, tiled=True)
+    partial_rows, gate_far = lax.optimization_barrier((partial_rows, gate_far))
+    gates = quarters(expert_gate_weight, gate_far)
+    line = req_count // 2
+    resid_own, arrived = pl.pallas_call(
+        functools.partial(middle_kernel, req_count, tp_count),
+        in_specs=[in_vmem] * 3,
+        out_specs=[in_vmem, in_place],
+        out_shape=[
+            jax.ShapeDtypeStruct((own_rows, width), bf16),
+            jax.ShapeDtypeStruct((req_count, own_rows, width), bf16),
+        ],
+        scratch_shapes=[
+            pltpu.VMEM((2, own_rows, width), bf16), pltpu.VMEM((own_rows, width), bf16),
+            pltpu.VMEM((own_rows, width), bf16), pltpu.VMEM((own_rows, width), bf16),
+            dma, dma((3,)), dma((3,)), dma((line,)), dma((line,)), dma((line,)), dma((line,)),
+        ],
+        compiler_params=pltpu.CompilerParams(
+            collective_id=2, has_side_effects=True, vmem_limit_bytes=32 << 20
+        ),
+        cost_estimate=pl.CostEstimate(
+            flops=0, bytes_accessed=200_000_000, transcendentals=0
+        ),
+        name="middle",
+    )(partial_rows.reshape(tp_count, own_rows, width), tokens, expert_norm_gain[None, :])
+    arrived = arrived.reshape(req_count * own_rows, width)
+    arrived, up_far, down_far = lax.optimization_barrier((arrived, up_far, down_far))
+    ups = quarters(expert_up_weight, up_far)
+    downs = quarters(expert_down_weight, down_far)
 
     local_experts = expert_gate_weight.shape[0]
     total_rows = req_count * own_rows
@@ -368,8 +598,21 @@
         ),
         name="experts",
     )(arrived, slot_of, expert_weight, *gates, *ups, *downs)
-    moe_own = lax.psum_scatter(moe, "req", scatter_dimension=0, tiled=True)
-    return (resid_own.astype(jnp.float32) + moe_own.astype(jnp.float32)).astype(jnp.bfloat16)
+    return pl.pallas_call(
+        functools.partial(closing_kernel, req_count),
+        in_specs=[in_vmem] * 2,
+        out_specs=in_vmem,
+        out_shape=jax.ShapeDtypeStruct((own_rows, width), bf16),
+        scratch_shapes=[pltpu.VMEM((line, own_rows, width), bf16)] * 3
+        + [dma((line,))] * 4,
+        compiler_params=pltpu.CompilerParams(
+            collective_id=3, has_side_effects=True, vmem_limit_bytes=48 << 20
+        ),
+        cost_estimate=pl.CostEstimate(
+            flops=0, bytes_accessed=150_000_000, transcendentals=0
+        ),
+        name="closing",
+    )(moe.reshape(req_count, own_rows, width), resid_own)
 
 
 def solution(mesh):

time: 402 us -> 309 us (0.77)
  waiting for transfers between devices: 271 us -> 7.32 us
  Pallas kernels: 48.5 us -> 270 us
  blocking collectives: 38.4 us -> 0 us
  between operations: 14.8 us -> 0.19 us
  other arithmetic: 15.9 us -> 8.03 us
  local copies, waits for them, and re-layouts: 9.15 us -> 15.3 us
    pallas_call x0 -> x3, Pallas kernels: none -> 223 us  [the longest x1 101 us: on_device(): pl.pallas_call(functools.partial(opening_kernel, req_count, tp_count, sto...]
    reduce_scatter x3 -> x0, waiting for transfers between devices: 167 us -> none  [the longest x1 74.6 us: on_device(): moe_own = lax.psum_scatter(moe, 'req', scatter_dimension=0, tiled=True)]
    ppermute x6, waiting for transfers between devices: 103 us -> 7.27 us  [the longest x3 7.26 us: quarters(): return [piece, far, near, lax.ppermute(far, 'tp', beside)]]
    all_gather x2 -> x0, blocking collectives: 38.4 us -> none  [the longest x1 32.3 us: on_device(): notes = lax.all_gather(notes, 'req', axis=0, tiled=False)]
    convert_element_type x8 -> x1, other arithmetic: 7.05 us -> 0.01 us  [on_device(): jnp.repeat(table_rows, ADAPTER_RANK).astype(jnp.float32)[:, None]]
    unnamed x30 -> x31, local copies, waits for them, and re-layouts: 4.81 us -> 11.5 us
  transfers between devices with their start and end apart: 14 -> 9, of which waited for: 7 -> 3; matrix products, arithmetic and copies ran while one was open for 2% -> 4% of each run, Pallas kernels for 0% -> 63%
where the time goes in v1:
time: 309 us; the launch traced here: 307 us
  Pallas kernels  270 us (87%)
  local copies, waits for them, and re-layouts  15.3 us (5%)
  other arithmetic  8.03 us (3%)
  waiting for transfers between devices  7.32 us (2%)
  starting transfers between devices  6.2 us (2%)
    pallas_call x1, Pallas kernels, on_device(): pl.pallas_call(functools.partial(opening_kernel, req_count, tp_count, sto...  101 us
    pallas_call x1, Pallas kernels, on_device(): pl.pallas_call(functools.partial(middle_kernel, req_count, tp_count), in_...  68.2 us
    pallas_call x1, Pallas kernels, on_device(): pl.pallas_call(functools.partial(closing_kernel, req_count), in_specs=[in...  53.2 us
    pallas_call x1, Pallas kernels, on_device(): pl.pallas_call(functools.partial(expert_kernel, slots), grid=(total_rows...  24.7 us
    pallas_call x1, Pallas kernels, on_device(): pl.pallas_call(functools.partial(attention_kernel, heads, kv_heads), grid...  16.4 us
    unnamed x31, local copies, waits for them, and re-layouts  11.5 us
    ppermute x3, waiting for transfers between devices, quarters(): return [piece, far, near, lax.ppermute(far, 'tp', beside)]  7.26 us
    pallas_call x1, Pallas kernels, on_device(): pl.pallas_call(functools.partial(projection_kernel, heads, kv_heads), gri...  6.73 us
  transfers between devices with their start and end apart: 9, of which 3 were waited for; matrix products, arithmetic and copies ran while one was open for 4% of the time, Pallas kernels for 63%

profile of v1, /device:TPU:0, one launch (start us, length us, event | category | flops | bytes accessed | tf_op | source)
XLA Modules:
  0.0 307.5 jit_solution(15201407006608119848)
XLA Ops:
  0.0 2.9 collective-permute-start
  3.5 1.7 collective-permute-start.2
  6.7 0.9 select_reduce_fusion.3
  7.6 0.9 convert_reduce_fusion.1
  10.9 1.3 broadcast_in_dim.89.gain_ref
  12.9 0.8 copy.23.spread_ref
  13.9 0.9 pad_maximum_fusion
  14.9 1.8 fusion.2
  16.7 101.2 %opening.1 = (bf16[4,128,1536]{2,1,0:T(8,128)(2,1)S(1)}, f32[8,16,128]{2,1,0:T(8,128)S(1)}, bf16[64,1536]{1,0:T(8,128)(2,1)S(1)}, bf16[64,384]{1,0:T(8,128)(2,1)S(1)}, bf16[64,128]{1,0:T(8,128)(2,1)S(1)}) custom-call(bf16[128,1536]{1,0:T(8,128)(2,1)S(1)} %copy-done.3, f32[80,128]{1,0:T(8,128)S(1)} %maximum_maximum_fusion.notes_ref, bf16[128,896]{1,0:T(8,128)(2,1)S(1)} %bitcast.45), custom_call_target="tpu_custom_call" | custom-call | bytes 90000000 | tf_op jit(solution)/shard_map/opening/pallas_call | solution.py:420
  118.0 1.1 copy-done.2
  121.1 6.7 %projections.1 = (bf16[6,512,128]{2,1,0:T(8,128)(2,1)}, bf16[512,128]{1,0:T(8,128)(2,1)}, bf16[512,128]{1,0:T(8,128)(2,1)}) custom-call(bf16[512,1536]{1,0:T(8,128)(2,1)} %bitcast.43, bf16[1,1536]{1,0:T(2,128)(2,1)} %broadcast_in_dim.89.gain_ref, bf16[1536,384]{1,0:T(8,128)(2,1)} %wq_ref.1, bf16[1536,128]{1,0:T(8,128)(2,1)} %wk_ref.1, ...), custom_call_target="tpu_custom_call" | custom-call | flops 1107296256 | bytes 6000000 | tf_op jit(solution)/shard_map/projections/pallas_call | solution.py:483
  127.9 1.2 copy-done.11
  129.1 1.1 copy-done.12
  130.2 0.9 copy-done.13
  131.1 0.9 copy-done.14
  132.0 16.4 %attention.1 = bf16[512,1536]{1,0:T(8,128)(2,1)S(1)} custom-call(s32[2,4]{1,0:T(2,128)S(1)} %pad_add_fusion.range_ref, bf16[6,512,128]{2,1,0:T(8,128)(2,1)S(1)} %copy-done.12, bf16[4096,128]{1,0:T(8,128)(2,1)S(1)} %copy-done.10, bf16[4096,128]{1,0:T(8,128)(2,1)S(1)} %copy-done.11, bf16[512,128]{1,0:T(8,128)(2,1)S(1)} %copy-done.13, ...), custom_call_target="tpu_custom_call" | custom-call | flops 10000000000 | bytes 6000000 | tf_op jit(solution)/shard_map/attention/pallas_call | solution.py:512
  148.9 68.2 %middle.1 = (bf16[128,1536]{1,0:T(8,128)(2,1)S(1)}, bf16[8,128,1536]{2,1,0:T(8,128)(2,1)S(1)}) custom-call(bf16[4,128,1536]{2,1,0:T(8,128)(2,1)S(1)} %bitcast.44, bf16[128,1536]{1,0:T(8,128)(2,1)S(1)} %copy-done.3, bf16[1,1536]{1,0:T(2,128)(2,1)S(1)} %broadcast_in_dim.94.gain_ref), custom_call_target="tpu_custom_call" | custom-call | bytes 200000000 | tf_op jit(solution)/shard_map/middle/pallas_call | solution.py:539
  217.1 1.7 copy-done.7
  219.7 2.8 collective-permute-done.4.refs_3_
  222.5 2.2 collective-permute-done.6.refs_7_
  224.7 2.2 collective-permute-done.8.refs_11_
  227.0 24.7 %experts.1 = bf16[1024,1536]{1,0:T(8,128)(2,1)} custom-call(bf16[1024,1536]{1,0:T(8,128)(2,1)} %bitcast.47, s32[4,1,1024]{2,1,0:T(1,128)S(1)} %bitcast.48, f32[4,1,1024]{2,1,0:T(1,128)S(1)} %bitcast.46, bf16[4,1536,128]{2,1,0:T(8,128)(2,1)S(1)} %copy-done.8, bf16[4,1536,128]{2,1,0:T(8,128)(2,1)} %collective-permute-done.refs_1_, ...), custom_call_target="tpu_custom_call" | custom-call | flops 12000000000 | bytes 26000000 | tf_op jit(solution)/shard_map/experts/pallas_call | solution.py:586
  251.7 1.9 copy-done.1
  253.6 53.2 %closing.1 = bf16[128,1536]{1,0:T(8,128)(2,1)S(1)} custom-call(bf16[8,128,1536]{2,1,0:T(8,128)(2,1)S(1)} %bitcast.42, bf16[128,1536]{1,0:T(8,128)(2,1)S(1)} %get-tuple-element.34.resid_ref), custom_call_target="tpu_custom_call" | custom-call | bytes 150000000 | tf_op jit(solution)/shard_map/closing/pallas_call | solution.py:601
  (64 shorter events, 9.5 us)
Async XLA Ops:
  0.0 13.9 %copy-start = (bf16[8,16,1536]{2,1,0:T(8,128)(2,1)S(1)}, bf16[8,16,1536]{2,1,0:T(8,128)(2,1)}, u32[]{:S(2)}) copy-start(bf16[8,16,1536]{2,1,0:T(8,128)(2,1)} %param.34) | copy-start | bytes 1179652
  0.0 16.7 %copy-start.3 = (bf16[128,1536]{1,0:T(8,128)(2,1)S(1)}, bf16[128,1536]{1,0:T(8,128)(2,1)}, u32[]{:S(2)}) copy-start(bf16[128,1536]{1,0:T(8,128)(2,1)} %tokens_ref.3) | copy-start | bytes 1179652
  0.0 148.4 %collective-permute-start = (bf16[4,1536,128]{2,1,0:T(8,128)(2,1)}, bf16[4,1536,128]{2,1,0:T(8,128)(2,1)}, u32[]{:S(2)}, u32[]{:S(2)}) collective-permute-start(bf16[4,1536,128]{2,1,0:T(8,128)(2,1)} %refs_0_.1), channel_id=1, source_target_pairs={{0,2},{1,3},{2,0},{3,1},{4,6},{5,7},{6,4},{7,5},{8,10},{9,11},{10,... | collective-permute-start | bytes 4718600 | tf_op jit(solution)/shard_map/ppermute | solution.py:402
  2.9 216.3 %collective-permute-start.3 = (bf16[4,1536,128]{2,1,0:T(8,128)(2,1)}, bf16[4,1536,128]{2,1,0:T(8,128)(2,1)}, u32[]{:S(2)}, u32[]{:S(2)}) collective-permute-start(bf16[4,1536,128]{2,1,0:T(8,128)(2,1)} %refs_0_.1), channel_id=1, source_target_pairs={{0,1},{1,0},{2,3},{3,2},{4,5},{5,4},{6,7},{7,6},{8,9},{9,8},{10,11... | collective-permute-start | bytes 4718600 | tf_op jit(solution)/shard_map/ppermute | solution.py:407
  2.9 215.8 %collective-permute-start.1 = (bf16[4,1536,128]{2,1,0:T(8,128)(2,1)}, bf16[4,1536,128]{2,1,0:T(8,128)(2,1)}, u32[]{:S(2)}, u32[]{:S(2)}) collective-permute-start(bf16[4,1536,128]{2,1,0:T(8,128)(2,1)} %refs_4_.1), channel_id=1, source_target_pairs={{0,2},{1,3},{2,0},{3,1},{4,6},{5,7},{6,4},{7,5},{8,10},{9,11},{10,... | collective-permute-start | bytes 4718600 | tf_op jit(solution)/shard_map/ppermute | solution.py:402
  3.1 216.5 %collective-permute-start.5 = (bf16[4,1536,128]{2,1,0:T(8,128)(2,1)}, bf16[4,1536,128]{2,1,0:T(8,128)(2,1)}, u32[]{:S(2)}, u32[]{:S(2)}) collective-permute-start(bf16[4,1536,128]{2,1,0:T(8,128)(2,1)} %refs_4_.1), channel_id=1, source_target_pairs={{0,1},{1,0},{2,3},{3,2},{4,5},{5,4},{6,7},{7,6},{8,9},{9,8},{10,11... | collective-permute-start | bytes 4718600 | tf_op jit(solution)/shard_map/ppermute | solution.py:407
  3.5 215.3 %collective-permute-start.2 = (bf16[4,128,1536]{2,1,0:T(8,128)(2,1)}, bf16[4,128,1536]{2,1,0:T(8,128)(2,1)}, u32[]{:S(2)}, u32[]{:S(2)}) collective-permute-start(bf16[4,128,1536]{2,1,0:T(8,128)(2,1)} %refs_8_.1), channel_id=1, source_target_pairs={{0,2},{1,3},{2,0},{3,1},{4,6},{5,7},{6,4},{7,5},{8,10},{9,11},{10,... | collective-permute-start | bytes 4718600 | tf_op jit(solution)/shard_map/ppermute | solution.py:402
  118.0 1.2 copy-start.2
  119.1 0.7 copy-start.4
  119.8 0.6 copy-start.5
  120.4 0.6 copy-start.6
  121.0 6.8 %copy-start.9 = (bf16[384,1536]{1,0:T(8,128)(2,1)S(1)}, bf16[384,1536]{1,0:T(8,128)(2,1)}, u32[]{:S(2)}) copy-start(bf16[384,1536]{1,0:T(8,128)(2,1)} %wo_ref.1) | copy-start | bytes 3538948
  121.1 6.8 %copy-start.10 = (bf16[4096,128]{1,0:T(8,128)(2,1)S(1)}, bf16[4096,128]{1,0:T(8,128)(2,1)}, u32[]{:S(2)}) copy-start(bf16[4096,128]{1,0:T(8,128)(2,1)} %ck_ref.1) | copy-start | bytes 3145732
  127.9 1.2 copy-start.11
  129.1 1.1 copy-start.12
  130.2 0.9 copy-start.13
  131.1 0.9 copy-start.14
  148.4 78.6 %copy-start.8 = (bf16[4,1536,128]{2,1,0:T(8,128)(2,1)S(1)}, bf16[4,1536,128]{2,1,0:T(8,128)(2,1)}, u32[]{:S(2)}) copy-start(bf16[4,1536,128]{2,1,0:T(8,128)(2,1)} %refs_0_.1) | copy-start | bytes 4718596
  148.4 71.3 %collective-permute-start.7 = (bf16[4,128,1536]{2,1,0:T(8,128)(2,1)}, bf16[4,128,1536]{2,1,0:T(8,128)(2,1)}, u32[]{:S(2)}, u32[]{:S(2)}) collective-permute-start(bf16[4,128,1536]{2,1,0:T(8,128)(2,1)} %refs_8_.1), channel_id=1, source_target_pairs={{0,1},{1,0},{2,3},{3,2},{4,5},{5,4},{6,7},{7,6},{8,9},{9,8},{10,11... | collective-permute-start | bytes 4718600 | tf_op jit(solution)/shard_map/ppermute | solution.py:407
  217.0 1.7 copy-start.7
  218.7 3.8 %collective-permute-start.4 = (bf16[4,1536,128]{2,1,0:T(8,128)(2,1)}, bf16[4,1536,128]{2,1,0:T(8,128)(2,1)}, u32[]{:S(2)}, u32[]{:S(2)}) collective-permute-start(bf16[4,1536,128]{2,1,0:T(8,128)(2,1)} %collective-permute-done.refs_1_), channel_id=1, source_target_pairs={{0,1},{1,0},{2,3},{3,2},{4,5},{5,4},{6,7},{7,6},{8,9},{9,8},{10,11... | collective-permute-start | bytes 4718600 | tf_op jit(solution)/shard_map/ppermute | solution.py:408
  218.7 6.0 %collective-permute-start.6 = (bf16[4,1536,128]{2,1,0:T(8,128)(2,1)}, bf16[4,1536,128]{2,1,0:T(8,128)(2,1)}, u32[]{:S(2)}, u32[]{:S(2)}) collective-permute-start(bf16[4,1536,128]{2,1,0:T(8,128)(2,1)} %collective-permute-done.1.refs_5_), channel_id=1, source_target_pairs={{0,1},{1,0},{2,3},{3,2},{4,5},{5,4},{6,7},{7,6},{8,9},{9,8},{10,11... | collective-permute-start | bytes 4718600 | tf_op jit(solution)/shard_map/ppermute | solution.py:408
  219.2 7.7 %collective-permute-start.8 = (bf16[4,128,1536]{2,1,0:T(8,128)(2,1)}, bf16[4,128,1536]{2,1,0:T(8,128)(2,1)}, u32[]{:S(2)}, u32[]{:S(2)}) collective-permute-start(bf16[4,128,1536]{2,1,0:T(8,128)(2,1)} %collective-permute-done.2.refs_9_), channel_id=1, source_target_pairs={{0,1},{1,0},{2,3},{3,2},{4,5},{5,4},{6,7},{7,6},{8,9},{9,8},{10,11... | collective-permute-start | bytes 4718600 | tf_op jit(solution)/shard_map/ppermute | solution.py:408
  251.7 1.9 copy-start.1

commit v2 on v1

--- a/solution.py
+++ b/solution.py
@@ -177,30 +177,38 @@
     return place + 1 - 2 * (place % 2)
 
 
+def token_kernel(tp_count, tokens_ref, group_ref, local_sem, x_send, x_recv):
+    here = lax.axis_index("tp")
+    beside, across = core_partner(here), (here + 2) % tp_count
+    greet([("tp", beside), ("tp", across)])
+    to_across = send_to(tokens_ref, group_ref.at[here], x_send.at[0], x_recv.at[0], "tp", across)
+    to_across.start()
+    to_beside = send_to(tokens_ref, group_ref.at[here], x_send.at[1], x_recv.at[1], "tp", beside)
+    to_beside.start()
+    own_copy = pltpu.make_async_copy(tokens_ref, group_ref.at[here], local_sem)
+    own_copy.start()
+    to_across.wait()
+    forward = send_to(group_ref.at[across], group_ref.at[across], x_send.at[2], x_recv.at[2], "tp",
+                      beside)
+    forward.start()
+    own_copy.wait()
+    to_beside.wait()
+    forward.wait()
+
+
 def opening_kernel(
-    req_count, tp_count, stored, tokens_ref, notes_ref, table_ref,
-    group_ref, all_notes_ref, down_ref, qup_ref, vup_ref,
-    noted, chosen, arrived, own_down, downs,
-    local_sem, x_send, x_recv, n_send, n_recv, a_send, a_recv, d_send, d_recv
+    req_count, stored, notes_ref, table_ref, all_notes_ref, down_ref, qup_ref, vup_ref,
+    noted, chosen, arrived, downs, n_send, n_recv, a_send, a_recv, d_send, d_recv
 ):
     me, here = lax.axis_index("req"), lax.axis_index("tp")
-    beside, across = core_partner(here), (here + 2) % tp_count
-    greet(
-        [("req", (me + step) % req_count) for step in range(1, req_count)]
-        + [("tp", (here + step) % tp_count) for step in range(1, tp_count)]
-    )
+    beside = core_partner(here)
+    greet([("req", (me + step) % req_count) for step in range(1, req_count)] + [("tp", beside)])
     note_copies = []
     for step in range(1, req_count):
         copy = send_to(notes_ref, noted.at[step], n_send.at[step], n_recv.at[step], "req",
                        (me + step) % req_count)
         copy.start()
         note_copies.append(copy)
-    own_copy = pltpu.make_async_copy(tokens_ref, group_ref.at[here], local_sem)
-    own_copy.start()
-    to_across = send_to(tokens_ref, group_ref.at[here], x_send.at[0], x_recv.at[0], "tp", across)
-    to_across.start()
-    to_beside = send_to(tokens_ref, group_ref.at[here], x_send.at[1], x_recv.at[1], "tp", beside)
-    to_beside.start()
 
     rows = GROUP_REQUESTS * ADAPTER_RANK
     depth = stored * ADAPTER_RANK
@@ -227,37 +235,27 @@
                        source)
         copy.start()
         adapter_copies.append(copy)
-    to_across.wait()
-    forward = send_to(group_ref.at[across], group_ref.at[across], x_send.at[2], x_recv.at[2], "tp",
-                      beside)
-    forward.start()
     for step in range(1, req_count):
         adapter_copies[step - 1].wait()
         total = total + arrived[step].astype(jnp.float32)
     total = total.astype(jnp.bfloat16)
-    down_width = own_down.shape[1]
+    down_width = downs.shape[2]
     query_width = qup_ref.shape[1]
-    own_down[...] = total[:, :down_width]
-    downs[here] = total[:, :down_width]
-    down_copies = []
-    for step in range(1, tp_count):
-        copy = send_to(own_down, downs.at[here], d_send.at[step], d_recv.at[step], "tp",
-                       (here + step) % tp_count)
-        copy.start()
-        down_copies.append(copy)
+    core = here % 2
+    downs[core] = total[:, :down_width]
+    copy = send_to(downs.at[core], downs.at[core], d_send, d_recv, "tp", beside)
+    copy.start()
     qup_ref[...] = total[:, down_width : down_width + query_width]
     vup_ref[...] = total[:, down_width + query_width :]
-    for copy in down_copies:
-        copy.wait()
-    down_ref[...] = jnp.concatenate([downs[i] for i in range(tp_count)], axis=1)
-    own_copy.wait()
-    to_beside.wait()
-    forward.wait()
+    copy.wait()
+    down_ref[...] = jnp.concatenate([downs[0], downs[1]], axis=1)
 
 
 def middle_kernel(
-    req_count, tp_count, partial_ref, tokens_ref, gain_ref, resid_ref, arrived_ref,
-    pair, joined, far, ffn, local_sem, p_send, p_recv, z_send, z_recv, f_send, f_recv
+    req_count, tp_count, partial_ref, tokens_ref, gain_ref, weight_ref,
+    resid_ref, arrived_ref, weight_far_ref, weight_near_ref, weight_far_near_ref,
+    pair, joined, far, ffn, local_sem, p_send, p_recv, z_send, z_recv, f_send, f_recv,
+    n_send, n_recv, w_send, w_recv, v_send, v_recv
 ):
     me, here = lax.axis_index("req"), lax.axis_index("tp")
     beside, across = core_partner(here), (here + 2) % tp_count
@@ -277,7 +275,16 @@
     joined[...] = (partial_ref[across].astype(f32) + pair[1].astype(f32)).astype(jnp.bfloat16)
     last = send_to(joined, far, p_send.at[2], p_recv.at[2], "tp", across)
     last.start()
+    pieces = weight_ref.shape[0]
+    far_copies = []
+    for piece in range(pieces):
+        copy = send_to(weight_ref.at[piece], weight_far_ref.at[piece], w_send.at[piece],
+                       w_recv.at[piece], "tp", across)
+        copy.start()
+        far_copies.append(copy)
     first.wait()
+    near_copy = send_to(weight_ref, weight_near_ref, n_send, n_recv, "tp", beside)
+    near_copy.start()
     own = partial_ref[here].astype(f32) + pair[0].astype(f32) + tokens_ref[...].astype(f32)
     last.wait()
     resid = (own + far[...].astype(f32)).astype(jnp.bfloat16)
@@ -301,9 +308,17 @@
                        f_recv.at[step], "req", partner)
         copy.start()
         forwards.append(copy)
+    near_forwards = []
+    for piece in range(pieces):
+        far_copies[piece].wait()
+        copy = send_to(weight_far_ref.at[piece], weight_far_near_ref.at[piece], v_send.at[piece],
+                       v_recv.at[piece], "tp", beside)
+        copy.start()
+        near_forwards.append(copy)
     own_copy.wait()
     to_partner.wait()
-    for copy in forwards:
+    near_copy.wait()
+    for copy in forwards + near_forwards:
         copy.wait()
 
 
@@ -395,34 +410,51 @@
     )
     notes = jnp.concatenate([own_routes.T.astype(jnp.float32), own_gates.T, wanted], axis=0)
 
-    across = [(i, i ^ 2) for i in range(tp_count)]
-    beside = [(i, i ^ 1) for i in range(tp_count)]
-
-    gate_far, up_far, down_far = (
-        lax.ppermute(piece, "tp", across)
-        for piece in (expert_gate_weight, expert_up_weight, expert_down_weight)
-    )
-
-    def quarters(piece, far):
-        near = lax.ppermute(piece, "tp", beside)
-        return [piece, far, near, lax.ppermute(far, "tp", beside)]
-
-    stored = adapter_down_maps.shape[0]
-    down_width = width // tp_count
-    down_part = lax.dynamic_slice_in_dim(adapter_down_maps, tp_place * down_width, down_width, 2)
-    table = jnp.concatenate([down_part, adapter_query_up, adapter_value_up], axis=2)
-    adapter_width = table.shape[2]
-    table = table.reshape(stored * ADAPTER_RANK, adapter_width)
     in_vmem = pl.BlockSpec(memory_space=pltpu.VMEM)
     in_place = pl.BlockSpec(memory_space=pl.ANY)
     dma = pltpu.SemaphoreType.DMA
     bf16 = jnp.bfloat16
-    group_x, notes, down_selected, query_up_selected, value_up_selected = pl.pallas_call(
-        functools.partial(opening_kernel, req_count, tp_count, stored),
-        in_specs=[in_vmem] * 3,
-        out_specs=[in_place] + [in_vmem] * 4,
+    group_x = pl.pallas_call(
+        functools.partial(token_kernel, tp_count),
+        in_specs=[in_vmem],
+        out_specs=in_place,
+        out_shape=jax.ShapeDtypeStruct((tp_count, own_rows, width), bf16),
+        scratch_shapes=[dma, dma((3,)), dma((3,))],
+        compiler_params=pltpu.CompilerParams(
+            collective_id=4, has_side_effects=True, vmem_limit_bytes=8 << 20
+        ),
+        cost_estimate=pl.CostEstimate(flops=0, bytes_accessed=40_000_000, transcendentals=0),
+        name="tokens",
+    )(tokens)
+    group_x, expert_gate_weight, expert_up_weight = lax.optimization_barrier(
+        (group_x, expert_gate_weight, expert_up_weight)
+    )
+
+    across = [(i, i ^ 2) for i in range(tp_count)]
+    beside = [(i, i ^ 1) for i in range(tp_count)]
+
+    gate_far, up_far = (
+        lax.ppermute(piece, "tp", across) for piece in (expert_gate_weight, expert_up_weight)
+    )
+
+    def quarters(piece, far):
+        near = lax.ppermute(piece, "tp", beside)
+        return [piece, far, near, lax.ppermute(far, "tp", beside)]
+
+    stored = adapter_down_maps.shape[0]
+    down_width = width // 2
+    down_part = lax.dynamic_slice_in_dim(
+        adapter_down_maps, tp_place % 2 * down_width, down_width, 2
+    )
+    table = jnp.concatenate([down_part, adapter_query_up, adapter_value_up], axis=2)
+    adapter_width = table.shape[2]
+    table = table.reshape(stored * ADAPTER_RANK, adapter_width)
+    notes, group_x = lax.optimization_barrier((notes, group_x))
+    notes, down_selected, query_up_selected, value_up_selected = pl.pallas_call(
+        functools.partial(opening_kernel, req_count, stored),
+        in_specs=[in_vmem] * 2,
+        out_specs=[in_vmem] * 4,
         out_shape=[
-            jax.ShapeDtypeStruct((tp_count, own_rows, width), bf16),
             jax.ShapeDtypeStruct((req_count, 2 * TOP, own_rows), jnp.float32),
             jax.ShapeDtypeStruct((low_rows, width), bf16),
             jax.ShapeDtypeStruct((low_rows, query_width), bf16),
@@ -432,19 +464,15 @@
             pltpu.VMEM((req_count,) + notes.shape, jnp.float32),
             pltpu.VMEM((req_count, low_rows, adapter_width), bf16),
             pltpu.VMEM((req_count, low_rows, adapter_width), bf16),
-            pltpu.VMEM((low_rows, down_width), bf16),
-            pltpu.VMEM((tp_count, low_rows, down_width), bf16),
-            dma, dma((3,)), dma((3,)), dma((req_count,)), dma((req_count,)),
-            dma((req_count,)), dma((req_count,)), dma((tp_count,)), dma((tp_count,)),
+            pltpu.VMEM((2, low_rows, down_width), bf16),
+            dma((req_count,)), dma((req_count,)), dma((req_count,)), dma((req_count,)), dma, dma,
         ],
         compiler_params=pltpu.CompilerParams(
             collective_id=1, has_side_effects=True, vmem_limit_bytes=32 << 20
         ),
-        cost_estimate=pl.CostEstimate(
-            flops=0, bytes_accessed=90_000_000, transcendentals=0
-        ),
+        cost_estimate=pl.CostEstimate(flops=0, bytes_accessed=90_000_000, transcendentals=0),
         name="opening",
-    )(tokens, notes, table)
+    )(notes, table)
     group_x = group_x.reshape(group_size, width)
     all_routes = notes[:, :TOP].astype(jnp.int32)
     all_gates = notes[:, TOP:]
@@ -536,18 +564,22 @@
     partial_rows, gate_far = lax.optimization_barrier((partial_rows, gate_far))
     gates = quarters(expert_gate_weight, gate_far)
     line = req_count // 2
-    resid_own, arrived = pl.pallas_call(
+    weight_shape = jax.ShapeDtypeStruct(expert_down_weight.shape, bf16)
+    pieces = expert_down_weight.shape[0]
+    resid_own, arrived, down_far, down_near, down_far_near = pl.pallas_call(
         functools.partial(middle_kernel, req_count, tp_count),
-        in_specs=[in_vmem] * 3,
-        out_specs=[in_vmem, in_place],
+        in_specs=[in_vmem] * 3 + [in_place],
+        out_specs=[in_vmem] + [in_place] * 4,
         out_shape=[
             jax.ShapeDtypeStruct((own_rows, width), bf16),
             jax.ShapeDtypeStruct((req_count, own_rows, width), bf16),
+            weight_shape, weight_shape, weight_shape,
         ],
         scratch_shapes=[
             pltpu.VMEM((2, own_rows, width), bf16), pltpu.VMEM((own_rows, width), bf16),
             pltpu.VMEM((own_rows, width), bf16), pltpu.VMEM((own_rows, width), bf16),
             dma, dma((3,)), dma((3,)), dma((line,)), dma((line,)), dma((line,)), dma((line,)),
+            dma, dma, dma((pieces,)), dma((pieces,)), dma((pieces,)), dma((pieces,)),
         ],
         compiler_params=pltpu.CompilerParams(
             collective_id=2, has_side_effects=True, vmem_limit_bytes=32 << 20
@@ -556,11 +588,12 @@
             flops=0, bytes_accessed=200_000_000, transcendentals=0
         ),
         name="middle",
-    )(partial_rows.reshape(tp_count, own_rows, width), tokens, expert_norm_gain[None, :])
+    )(partial_rows.reshape(tp_count, own_rows, width), tokens, expert_norm_gain[None, :],
+      expert_down_weight)
     arrived = arrived.reshape(req_count * own_rows, width)
-    arrived, up_far, down_far = lax.optimization_barrier((arrived, up_far, down_far))
+    arrived, up_far = lax.optimization_barrier((arrived, up_far))
     ups = quarters(expert_up_weight, up_far)
-    downs = quarters(expert_down_weight, down_far)
+    downs = [expert_down_weight, down_far, down_near, down_far_near]
 
     local_experts = expert_gate_weight.shape[0]
     total_rows = req_count * own_rows

time: 309 us -> 255 us (0.83)
  Pallas kernels: 270 us -> 224 us
  local copies, waits for them, and re-layouts: 15.3 us -> 19.7 us
  other arithmetic: 8.03 us -> 3.64 us
  waiting for transfers between devices: 7.32 us -> 3.37 us
  starting transfers between devices: 6.2 us -> 2.83 us
    pallas_call x1 -> x2, Pallas kernels: 101 us -> 58.7 us  [the longest x1 44.5 us: on_device(): pl.pallas_call(functools.partial(opening_kernel, req_count, stored), in_s...]
    pallas_call x1, Pallas kernels: 68.2 us -> 58 us  [on_device(): pl.pallas_call(functools.partial(middle_kernel, req_count, tp_count), in_...]
    unnamed x31 -> x55, local copies, waits for them, and re-layouts: 11.5 us -> 17.3 us
    ppermute x3 -> x2, waiting for transfers between devices: 7.26 us -> 3.32 us  [quarters(): return [piece, far, near, lax.ppermute(far, 'tp', beside)]]
    pallas_call x1, Pallas kernels: 16.4 us -> 19.9 us  [on_device(): pl.pallas_call(functools.partial(attention_kernel, heads, kv_heads), grid...]
  transfers between devices with their start and end apart: 9 -> 6, of which waited for: 3 -> 1; matrix products, arithmetic and copies ran while one was open for 4% -> 2% of each run, Pallas kernels for 63% -> 51%
where the time goes in v2:
time: 255 us; the launch traced here: 254 us
  Pallas kernels  224 us (88%)
  local copies, waits for them, and re-layouts  19.7 us (8%)
  other arithmetic  3.64 us (1%)
  waiting for transfers between devices  3.37 us (1%)
  starting transfers between devices  2.83 us (1%)
    pallas_call x1, Pallas kernels, on_device(): pl.pallas_call(functools.partial(middle_kernel, req_count, tp_count), in_...  58 us
    pallas_call x1, Pallas kernels, on_device(): pl.pallas_call(functools.partial(closing_kernel, req_count), in_specs=[in...  55.8 us
    pallas_call x1, Pallas kernels, on_device(): pl.pallas_call(functools.partial(opening_kernel, req_count, stored), in_s...  44.5 us
    pallas_call x1, Pallas kernels, on_device(): pl.pallas_call(functools.partial(expert_kernel, slots), grid=(total_rows...  25 us
    pallas_call x1, Pallas kernels, on_device(): pl.pallas_call(functools.partial(attention_kernel, heads, kv_heads), grid...  19.9 us
    unnamed x55, local copies, waits for them, and re-layouts  17.3 us
    pallas_call x1, Pallas kernels, on_device(): pl.pallas_call(functools.partial(token_kernel, tp_count), in_specs=[in_vm...  14.2 us
    pallas_call x1, Pallas kernels, on_device(): pl.pallas_call(functools.partial(projection_kernel, heads, kv_heads), gri...  6.65 us
  transfers between devices with their start and end apart: 6, of which 1 were waited for; matrix products, arithmetic and copies ran while one was open for 2% of the time, Pallas kernels for 51%

profile of v2, /device:TPU:0, one launch (start us, length us, event | category | flops | bytes accessed | tf_op | source)
XLA Modules:
  0.0 254.0 jit_solution(13257507342359440772)
XLA Ops:
  0.0 1.0 copy-done.4
  1.1 14.2 %tokens.1 = bf16[4,128,1536]{2,1,0:T(8,128)(2,1)S(1)} custom-call(bf16[128,1536]{1,0:T(8,128)(2,1)S(1)} %copy-done.4), custom_call_target="tpu_custom_call" | custom-call | bytes 40000000 | tf_op jit(solution)/shard_map/tokens/pallas_call | solution.py:417
  15.3 1.1 copy-done.1
  16.8 1.1 collective-permute-start
  17.9 1.0 collective-permute-start.1
  21.8 0.8 copy.23.spread_ref
  22.9 44.5 %opening.1 = (f32[8,16,128]{2,1,0:T(8,128)S(1)}, bf16[64,1536]{1,0:T(8,128)(2,1)S(1)}, bf16[64,384]{1,0:T(8,128)(2,1)S(1)}, bf16[64,128]{1,0:T(8,128)(2,1)S(1)}) custom-call(f32[80,128]{1,0:T(8,128)S(1)} %maximum_maximum_fusion.notes_ref, bf16[128,1280]{1,0:T(8,128)(2,1)S(1)} %bitcast.45), custom_call_target="tpu_custom_call" | custom-call | bytes 90000000 | tf_op jit(solution)/shard_map/opening/pallas_call | solution.py:453
  69.3 1.8 fusion.2
  71.2 6.6 %projections.1 = (bf16[6,512,128]{2,1,0:T(8,128)(2,1)}, bf16[512,128]{1,0:T(8,128)(2,1)}, bf16[512,128]{1,0:T(8,128)(2,1)}) custom-call(bf16[512,1536]{1,0:T(8,128)(2,1)} %bitcast.42, bf16[1,1536]{1,0:T(2,128)(2,1)} %broadcast_in_dim.89.gain_ref, bf16[1536,384]{1,0:T(8,128)(2,1)} %wq_ref.1, bf16[1536,128]{1,0:T(8,128)(2,1)} %wk_ref.1, ...), custom_call_target="tpu_custom_call" | custom-call | flops 1107296256 | bytes 6000000 | tf_op jit(solution)/shard_map/projections/pallas_call | solution.py:511
  77.9 1.3 copy-done.13
  79.1 1.2 copy-done.15
  80.4 1.1 copy-done.16
  81.5 0.9 copy-done.17
  82.4 0.9 copy-done.18
  83.3 19.9 %attention.1 = bf16[512,1536]{1,0:T(8,128)(2,1)S(1)} custom-call(s32[2,4]{1,0:T(2,128)S(1)} %pad_add_fusion.range_ref, bf16[6,512,128]{2,1,0:T(8,128)(2,1)S(1)} %copy-done.16, bf16[4096,128]{1,0:T(8,128)(2,1)S(1)} %copy-done.14, bf16[4096,128]{1,0:T(8,128)(2,1)S(1)} %copy-done.15, bf16[512,128]{1,0:T(8,128)(2,1)S(1)} %copy-done.17, ...), custom_call_target="tpu_custom_call" | custom-call | flops 10000000000 | bytes 6000000 | tf_op jit(solution)/shard_map/attention/pallas_call | solution.py:540
  103.6 58.0 %middle.1 = (bf16[128,1536]{1,0:T(8,128)(2,1)S(1)}, bf16[8,128,1536]{2,1,0:T(8,128)(2,1)S(1)}, bf16[4,128,1536]{2,1,0:T(8,128)(2,1)S(1)}, bf16[4,128,1536]{2,1,0:T(8,128)(2,1)S(1)}, bf16[4,128,1536]{2,1,0:T(8,128)(2,1)S(1)}) custom-call(bf16[4,128,1536]{2,1,0:T(8,128)(2,1)S(1)} %bitcast.44, bf16[128,1536]{1,0:T(8,128)(2,1)S(1)} %copy-done.5, ...), custom_call_target="tpu_custom_call" | custom-call | bytes 200000000 | tf_op jit(solution)/shard_map/middle/pallas_call | solution.py:569
  161.7 1.6 copy-done.9
  163.3 1.1 copy-done.10
  164.4 1.2 copy-done.11
  165.6 1.2 copy-done.12
  167.2 3.3 %collective-permute-done.5.refs_7_ = bf16[4,1536,128]{2,1,0:T(8,128)(2,1)} collective-permute-done((bf16[4,1536,128]{2,1,0:T(8,128)(2,1)}, bf16[4,1536,128]{2,1,0:T(8,128)(2,1)}, u32[]{:S(2)}, u32[]{:S(2)}) %collective-permute-start.5) | collective-permute-done | bytes 1572896 | tf_op jit(solution)/shard_map/ppermute | solution.py:442
  170.5 25.0 %experts.1 = bf16[1024,1536]{1,0:T(8,128)(2,1)} custom-call(bf16[1024,1536]{1,0:T(8,128)(2,1)} %bitcast.47, s32[4,1,1024]{2,1,0:T(1,128)S(1)} %bitcast.48, f32[4,1,1024]{2,1,0:T(1,128)S(1)} %bitcast.46, bf16[4,1536,128]{2,1,0:T(8,128)(2,1)} %refs_0_, bf16[4,1536,128]{2,1,0:T(8,128)(2,1)} %collective-permute-done.refs_1_, ...), custom_call_target="tpu_custom_call" | custom-call | flops 12000000000 | bytes 26000000 | tf_op jit(solution)/shard_map/experts/pallas_call | solution.py:619
  195.5 1.9 copy-done.2
  197.4 55.8 %closing.1 = bf16[128,1536]{1,0:T(8,128)(2,1)S(1)} custom-call(bf16[8,128,1536]{2,1,0:T(8,128)(2,1)S(1)} %bitcast.43, bf16[128,1536]{1,0:T(8,128)(2,1)S(1)} %get-tuple-element.46.resid_ref), custom_call_target="tpu_custom_call" | custom-call | bytes 150000000 | tf_op jit(solution)/shard_map/closing/pallas_call | solution.py:634
  (83 shorter events, 7.1 us)
Async XLA Ops:
  0.0 22.8 %copy-start = (bf16[8,16,1536]{2,1,0:T(8,128)(2,1)S(1)}, bf16[8,16,1536]{2,1,0:T(8,128)(2,1)}, u32[]{:S(2)}) copy-start(bf16[8,16,1536]{2,1,0:T(8,128)(2,1)} %param.34) | copy-start | bytes 1179652
  1.1 17.8 %copy-start.21 = (s32[1,512]{1,0:T(1,128)S(1)}, s32[1,512]{1,0:T(1,128)}, u32[]{:S(2)}) copy-start(s32[1,512]{1,0:T(1,128)} %param.30) | copy-start | bytes 6148
  1.1 17.9 %copy-start.25 = (s32[64]{0:T(128)S(1)}, s32[64]{0:T(128)}, u32[]{:S(2)}) copy-start(s32[64]{0:T(128)} %param.33) | copy-start | bytes 772
  1.1 17.9 %copy-start.26 = (s32[1,4]{1,0:T(1,128)S(1)}, s32[1,4]{1,0:T(1,128)}, u32[]{:S(2)}) copy-start(s32[1,4]{1,0:T(1,128)} %param.32) | copy-start | bytes 52
  1.1 18.1 %copy-start.22 = (s32[1,4096]{1,0:T(1,128)S(1)}, s32[1,4096]{1,0:T(1,128)}, u32[]{:S(2)}) copy-start(s32[1,4096]{1,0:T(1,128)} %param.31) | copy-start | bytes 49156
  1.1 20.1 %copy-start.23 = (bf16[1536]{0:T(1024)(128)(2,1)S(1)}, bf16[1536]{0:T(1024)(128)(2,1)}, u32[]{:S(2)}) copy-start(bf16[1536]{0:T(1024)(128)(2,1)} %param.22) | copy-start | bytes 9220
  1.1 20.7 %copy-start.24 = (bf16[1536]{0:T(1024)(128)(2,1)S(1)}, bf16[1536]{0:T(1024)(128)(2,1)}, u32[]{:S(2)}) copy-start(bf16[1536]{0:T(1024)(128)(2,1)} %param.23) | copy-start | bytes 9220
  1.1 21.8 %copy-start.19 = (bf16[8,16,384]{2,1,0:T(8,128)(2,1)S(1)}, bf16[8,16,384]{2,1,0:T(8,128)(2,1)}, u32[]{:S(2)}) copy-start(bf16[8,16,384]{2,1,0:T(8,128)(2,1)} %param.35) | copy-start | bytes 294916
  1.1 21.8 %copy-start.20 = (bf16[8,16,128]{2,1,0:T(8,128)(2,1)S(1)}, bf16[8,16,128]{2,1,0:T(8,128)(2,1)}, u32[]{:S(2)}) copy-start(bf16[8,16,128]{2,1,0:T(8,128)(2,1)} %param.36) | copy-start | bytes 98308
  16.4 150.7 %collective-permute-start.2 = (bf16[4,1536,128]{2,1,0:T(8,128)(2,1)}, bf16[4,1536,128]{2,1,0:T(8,128)(2,1)}, u32[]{:S(2)}, u32[]{:S(2)}) collective-permute-start(bf16[4,1536,128]{2,1,0:T(8,128)(2,1)} %refs_0_), channel_id=1, source_target_pairs={{0,1},{1,0},{2,3},{3,2},{4,5},{5,4},{6,7},{7,6},{8,9},{9,8},{10,11... | collective-permute-start | bytes 4718600 | tf_op jit(solution)/shard_map/ppermute | solution.py:441
  16.8 86.4 %collective-permute-start = (bf16[4,1536,128]{2,1,0:T(8,128)(2,1)}, bf16[4,1536,128]{2,1,0:T(8,128)(2,1)}, u32[]{:S(2)}, u32[]{:S(2)}) collective-permute-start(bf16[4,1536,128]{2,1,0:T(8,128)(2,1)} %refs_0_), channel_id=1, source_target_pairs={{0,2},{1,3},{2,0},{3,1},{4,6},{5,7},{6,4},{7,5},{8,10},{9,11},{10,... | collective-permute-start | bytes 4718600 | tf_op jit(solution)/shard_map/ppermute | solution.py:437
  17.9 149.3 %collective-permute-start.4 = (bf16[4,1536,128]{2,1,0:T(8,128)(2,1)}, bf16[4,1536,128]{2,1,0:T(8,128)(2,1)}, u32[]{:S(2)}, u32[]{:S(2)}) collective-permute-start(bf16[4,1536,128]{2,1,0:T(8,128)(2,1)} %refs_4_), channel_id=1, source_target_pairs={{0,1},{1,0},{2,3},{3,2},{4,5},{5,4},{6,7},{7,6},{8,9},{9,8},{10,11... | collective-permute-start | bytes 4718600 | tf_op jit(solution)/shard_map/ppermute | solution.py:441
  17.9 148.9 %collective-permute-start.1 = (bf16[4,1536,128]{2,1,0:T(8,128)(2,1)}, bf16[4,1536,128]{2,1,0:T(8,128)(2,1)}, u32[]{:S(2)}, u32[]{:S(2)}) collective-permute-start(bf16[4,1536,128]{2,1,0:T(8,128)(2,1)} %refs_4_), channel_id=1, source_target_pairs={{0,2},{1,3},{2,0},{3,1},{4,6},{5,7},{6,4},{7,5},{8,10},{9,11},{10,... | collective-permute-start | bytes 4718600 | tf_op jit(solution)/shard_map/ppermute | solution.py:437
  71.1 6.7 %copy-start.14 = (bf16[4096,128]{1,0:T(8,128)(2,1)S(1)}, bf16[4096,128]{1,0:T(8,128)(2,1)}, u32[]{:S(2)}) copy-start(bf16[4096,128]{1,0:T(8,128)(2,1)} %ck_ref.1) | copy-start | bytes 3145732
  77.9 1.3 copy-start.13
  79.1 1.2 copy-start.15
  83.3 20.3 %copy-start.3 = (bf16[4,128,1536]{2,1,0:T(8,128)(2,1)S(1)}, bf16[4,128,1536]{2,1,0:T(8,128)(2,1)}, u32[]{:S(2)}) copy-start(bf16[4,128,1536]{2,1,0:T(8,128)(2,1)} %refs_8_.1) | copy-start | bytes 4718596
  83.3 20.3 %copy-start.5 = (bf16[128,1536]{1,0:T(8,128)(2,1)S(1)}, bf16[128,1536]{1,0:T(8,128)(2,1)}, u32[]{:S(2)}) copy-start(bf16[128,1536]{1,0:T(8,128)(2,1)} %tokens_ref.3) | copy-start | bytes 1179652
  103.2 64.0 %collective-permute-start.3 = (bf16[4,1536,128]{2,1,0:T(8,128)(2,1)}, bf16[4,1536,128]{2,1,0:T(8,128)(2,1)}, u32[]{:S(2)}, u32[]{:S(2)}) collective-permute-start(bf16[4,1536,128]{2,1,0:T(8,128)(2,1)} %collective-permute-done.refs_1_), channel_id=1, source_target_pairs={{0,1},{1,0},{2,3},{3,2},{4,5},{5,4},{6,7},{7,6},{8,9},{9,8},{10,11... | collective-permute-start | bytes 4718600 | tf_op jit(solution)/shard_map/ppermute | solution.py:442
  161.6 1.6 copy-start.9
  164.4 1.2 copy-start.11
  165.6 1.2 copy-start.12
  166.8 3.8 %collective-permute-start.5 = (bf16[4,1536,128]{2,1,0:T(8,128)(2,1)}, bf16[4,1536,128]{2,1,0:T(8,128)(2,1)}, u32[]{:S(2)}, u32[]{:S(2)}) collective-permute-start(bf16[4,1536,128]{2,1,0:T(8,128)(2,1)} %collective-permute-done.1.refs_5_), channel_id=1, source_target_pairs={{0,1},{1,0},{2,3},{3,2},{4,5},{5,4},{6,7},{7,6},{8,9},{9,8},{10,11... | collective-permute-start | bytes 4718600 | tf_op jit(solution)/shard_map/ppermute | solution.py:442
  195.5 1.9 copy-start.2
  (9 other events, 8.2 us)
